TPU v7x, 32 devices: a whole 2x2x4 slice. The times are simulated.
32 devices in a mesh: ctx: 4 (over y, core), exp: 8 (over z, x).
Axes of the slice: x: 2, y: 2, z: 4, core: 2. Of those that a mesh axis runs over, the one named last changes fastest.
Arguments:
- stream: bfloat16 [8, 512, 2048], P('exp', 'ctx'), may hold values from -16 to 16
- queries: bfloat16 [8, 512, 1024], P('exp', 'ctx'), may hold values from -6 to 6
- key_proj: bfloat16 [8, 512, 1024], P('exp', 'ctx'), may hold values from -6 to 6
- value_proj: bfloat16 [8, 512, 2048], P('exp', 'ctx'), may hold values from -6 to 6
- gate_proj: bfloat16 [8, 512, 2048], P('exp', 'ctx'), may hold values from -6 to 6
- write_rate: float32 [8, 512, 16], P('exp', 'ctx'), may hold values from 0.02 to 0.3
- log_decay: float32 [8, 512, 16], P('exp', 'ctx'), may hold values from -1 to 0
- init_state: float32 [8, 16, 128, 128], P('exp'), may hold values from -0.6 to 0.6
- head_gain: float32 [128], replicated, may hold values from 0.1 to 1.9
- out_weight: bfloat16 [2048, 2048], P(None, 'ctx'), may hold values from -0.125 to 0.125
- moe_gain: float32 [2048], replicated, may hold values from 0.1 to 1.9
- routes: int32 [8, 512, 10], P('exp', 'ctx'), may hold values from 0 to 31, as said below
- route_gate: float32 [8, 512, 10], P('exp', 'ctx'), may hold values from 0.05 to 0.2
- expert_up: bfloat16 [32, 2048, 1024], P(('ctx', 'exp')), may hold values from -0.125 to 0.125
- expert_down: bfloat16 [32, 512, 2048], P(('ctx', 'exp')), may hold values from -0.25 to 0.25
Outputs:
- mixed: bfloat16 [8, 512, 2048], P('exp', 'ctx')
- moe_output: bfloat16 [8, 512, 2048], P('exp', 'ctx')
Inputs may be any that keep to these rules, and one draw needn't show every extreme that they name: `routes`: within the 128 tokens of one device the 10 ids of a token differ, and every expert id is named exactly 128 * 10 / 32 times.
All inputs are finite; a program needn't handle non-finite values.
Results may differ from a plain program's by a relative error of at most 0.019.
Values may be sent and summed in bfloat16 or wider, within the bound.
A program may use at most 128 MiB of HBM per device.

v0:
```python
import jax
import jax.numpy as jnp
from jax import lax
from jax.sharding import PartitionSpec as P

D = 2048
HK = 8
OUTPUT_CHANNELS = 16
DK = 128
DV = 128
FF = 512
TOP = 10


def shifted(value, axis, steps):
    count = lax.axis_size(axis)
    first, last = (max(0, -steps), min(count, count - steps))
    return lax.ppermute(value, axis, [(source, source + steps) for source in range(first, last)])


def on_device(
    stream,
    queries,
    key_proj,
    value_proj,
    gate_proj,
    write_rate,
    log_decay,
    init_state,
    head_gain,
    out_weight,
    moe_gain,
    routes,
    route_gate,
    expert_up,
    expert_down,
):
    highest = lax.Precision.HIGHEST
    length = stream.shape[1]
    repeat = OUTPUT_CHANNELS // HK
    query_loc = jnp.repeat(
        queries[0].astype(jnp.float32).reshape(length, HK, DK), repeat, axis=1
    ).transpose(1, 0, 2)
    key_loc = key_proj[0].astype(jnp.float32).reshape(length, HK, DK)
    key_loc = key_loc * lax.rsqrt(jnp.sum(key_loc * key_loc, axis=-1, keepdims=True) + 1e-06)
    key_loc = jnp.repeat(key_loc, repeat, axis=1).transpose(1, 0, 2)
    value_loc = (
        value_proj[0].astype(jnp.float32).reshape(length, OUTPUT_CHANNELS, DV).transpose(1, 0, 2)
    )
    rate_loc = write_rate[0].T
    cumulative = jnp.cumsum(log_decay[0], axis=0).T
    later = lax.broadcasted_iota(jnp.int32, (length, length), 0)
    earlier = lax.broadcasted_iota(jnp.int32, (length, length), 1)
    strict = later > earlier
    inclusive = later >= earlier
    spread = jnp.exp(
        jnp.where(inclusive[None], cumulative[:, :, None] - cumulative[:, None, :], 0.0)
    )
    key_key = jnp.einsum("htd,hsd->hts", key_loc, key_loc, precision=highest)
    query_key = jnp.einsum("htd,hsd->hts", query_loc, key_loc, precision=highest)
    lower_part = jnp.where(strict[None], rate_loc[:, :, None] * spread * key_key, 0.0)
    attend = jnp.where(inclusive[None], spread * query_key, 0.0)
    decay_now = jnp.exp(cumulative)
    right_side = jnp.concatenate(
        [rate_loc[:, :, None] * value_loc, (rate_loc * decay_now)[:, :, None] * key_loc], axis=-1
    )
    unit_lower = jnp.eye(length, dtype=jnp.float32)[None] + lower_part
    solved = jax.scipy.linalg.solve_triangular(
        unit_lower, right_side, lower=True, unit_diagonal=True
    )
    update = solved[:, :, :DV]
    w_rows = solved[:, :, DV:]
    intra = jnp.einsum("hts,hsv->htv", attend, update, precision=highest)
    query_eff = decay_now[:, :, None] * query_loc - jnp.einsum(
        "hts,hsd->htd", attend, w_rows, precision=highest
    )
    key_tail = jnp.exp(cumulative[:, -1:] - cumulative)[:, :, None] * key_loc
    eye_key = jnp.eye(DK, dtype=jnp.float32)[None]
    transit = decay_now[:, -1][:, None, None] * eye_key - jnp.einsum(
        "htd,hte->hde", key_tail, w_rows, precision=highest
    )
    carry_add = jnp.einsum("htd,htv->hdv", key_tail, update, precision=highest)
    first_state = init_state[0]
    position = lax.axis_index("ctx")

    def relay_step(turn, start_state):
        end_state = jnp.einsum("hde,hev->hdv", transit, start_state, precision=highest) + carry_add
        incoming = shifted(end_state, "ctx", 1)
        return jnp.where(position == 0, first_state, incoming)

    start_state = lax.fori_loop(0, lax.axis_size("ctx") - 1, relay_step, first_state)
    head_out = intra + jnp.einsum("htd,hdv->htv", query_eff, start_state, precision=highest)
    gate_loc = (
        gate_proj[0].astype(jnp.float32).reshape(length, OUTPUT_CHANNELS, DV).transpose(1, 0, 2)
    )
    square_mean = jnp.mean(head_out * head_out, axis=-1, keepdims=True)
    gated = head_out * lax.rsqrt(square_mean + 1e-06) * head_gain * jax.nn.silu(gate_loc)
    gated = gated.transpose(1, 0, 2).reshape(length, OUTPUT_CHANNELS * DV).astype(jnp.bfloat16)
    column_block = jnp.dot(
        lax.all_gather(gated, "ctx", axis=0, tiled=True),
        out_weight,
        preferred_element_type=jnp.float32,
    )
    attn = lax.all_to_all(column_block, "ctx", split_axis=0, concat_axis=1, tiled=True)
    mixed = (stream[0].astype(jnp.float32) + attn).astype(jnp.bfloat16)
    mixed_f = mixed.astype(jnp.float32)
    moe_in = (
        mixed_f * lax.rsqrt(jnp.mean(mixed_f * mixed_f, axis=-1, keepdims=True) + 1e-06) * moe_gain
    ).astype(jnp.bfloat16)
    ctx_count = lax.axis_size("ctx")
    exp_count = lax.axis_size("exp")
    local_experts = expert_up.shape[0]
    flat_routes = routes[0].reshape(-1)
    order = jnp.argsort(flat_routes, stable=True)
    per_owner = length * TOP // (ctx_count * exp_count)
    outgoing = moe_in[order // TOP].reshape(ctx_count, exp_count, per_owner, D)
    arrived = lax.all_to_all(
        lax.all_to_all(outgoing, "ctx", split_axis=0, concat_axis=0, tiled=True),
        "exp",
        split_axis=1,
        concat_axis=1,
        tiled=True,
    )
    slot_count = per_owner // local_experts
    grouped = arrived.reshape(ctx_count * exp_count, local_experts, slot_count, D).transpose(
        1, 0, 2, 3
    )
    grouped = grouped.reshape(local_experts, ctx_count * exp_count * slot_count, D)
    pre = jnp.einsum("erd,edf->erf", grouped, expert_up, preferred_element_type=jnp.float32)
    hidden = (jax.nn.silu(pre[:, :, :FF]) * pre[:, :, FF:]).astype(jnp.bfloat16)
    produced = jnp.einsum(
        "erf,efd->erd", hidden, expert_down, preferred_element_type=jnp.float32
    ).astype(jnp.bfloat16)
    produced = produced.reshape(local_experts, ctx_count * exp_count, slot_count, D).transpose(
        1, 0, 2, 3
    )
    produced = produced.reshape(ctx_count, exp_count, per_owner, D)
    returned = lax.all_to_all(
        lax.all_to_all(produced, "ctx", split_axis=0, concat_axis=0, tiled=True),
        "exp",
        split_axis=1,
        concat_axis=1,
        tiled=True,
    )
    inverse = (
        jnp.zeros((length * TOP,), jnp.int32)
        .at[order]
        .set(jnp.arange(length * TOP, dtype=jnp.int32))
    )
    per_route = returned.reshape(length * TOP, D)[inverse].reshape(length, TOP, D)
    combined = jnp.einsum("tj,tjd->td", route_gate[0], per_route.astype(jnp.float32))
    moe_output = combined.astype(jnp.bfloat16)
    return (mixed[None], moe_output[None])


def solution(mesh):
    return jax.shard_map(
        on_device,
        mesh=mesh,
        in_specs=(
            P("exp", "ctx", None),
            P("exp", "ctx", None),
            P("exp", "ctx", None),
            P("exp", "ctx", None),
            P("exp", "ctx", None),
            P("exp", "ctx", None),
            P("exp", "ctx", None),
            P("exp", None, None, None),
            P(),
            P(None, "ctx"),
            P(),
            P("exp", "ctx", None),
            P("exp", "ctx", None),
            P(("ctx", "exp"), None, None),
            P(("ctx", "exp"), None, None),
        ),
        out_specs=(P("exp", "ctx", None), P("exp", "ctx", None)),
        check_vma=False,
    )
```

profile of v0, /device:TPU:5, one launch (start us, length us, event | category | flops | bytes accessed | tf_op | source)
XLA Modules:
  0.0 753.7 jit_solution(18360218965852849136)
XLA Ops:
  20.5 3.4 fusion.13
  23.9 158.8 %custom-call.4 = f32[16,1,128,128]{2,3,1,0:T(8,128)} custom-call(f32[16,1,128,128]{3,2,1,0:T(8,128)} %fusion.13), custom_call_target="InvertDiagBlocksLowerTriangular" | custom-call | tf_op jit(solution)/shard_map/jit(_solve_triangular)/vmap()/triangular_solve | solution.py:68
  187.5 2.9 fusion.26
  194.1 4.5 fusion.24
  198.7 3.0 convolution_subtract_fusion
  203.9 56.0 %while.12 = (s32[]{:T(128)}, f32[16,128,128]{2,1,0:T(8,128)S(1)}, pred[]{:T(512)}, f32[16,128,128]{2,1,0:T(8,128)}, f32[16,128,128]{2,1,0:T(8,128)}, /*index=5*/f32[16,128,128]{2,1,0:T(8,128)}, s32[]{:T(128)}) while((s32[]{:T(128)}, f32[16,128,128]{2,1,0:T(8,128)S(1)}, pred[]{:T(512)}, f32[16,128,128]{2,1,0:T(8,128)}, ...), condition=%wide.region_3.4_spmd, body=%wide.region_2.3_spmd.sunk | while | flops 403177472 | bytes 15728786 | solution.py:91
  203.9 3.7 convolution_add_fusion.3
  208.9 3.7 collective-permute-done
  214.9 3.7 convolution_add_fusion.3
  219.9 15.0 %collective-permute-done = f32[16,128,128]{2,1,0:T(8,128)S(1)} collective-permute-done((f32[16,128,128]{2,1,0:T(8,128)}, f32[16,128,128]{2,1,0:T(8,128)S(1)}, u32[]{:S(2)}, u32[]{:S(2)}) %collective-permute-start) | collective-permute-done | bytes 1048608 | tf_op jit(solution)/shard_map/while/body/eval_jaxpr/ppermute | solution.py:18
  237.3 3.7 convolution_add_fusion.3
  242.2 15.0 %collective-permute-done = f32[16,128,128]{2,1,0:T(8,128)S(1)} collective-permute-done((f32[16,128,128]{2,1,0:T(8,128)}, f32[16,128,128]{2,1,0:T(8,128)S(1)}, u32[]{:S(2)}, u32[]{:S(2)}) %collective-permute-start) | collective-permute-done | bytes 1048608 | tf_op jit(solution)/shard_map/while/body/eval_jaxpr/ppermute | solution.py:18
  259.9 3.5 multiply_reduce_fusion.1
  264.6 34.8 %all-gather.2.cloned.1.call-done = bf16[512,2048]{0,1:T(8,128)(2,1)} async-done(((bf16[128,2048]{0,1:T(8,128)(2,1)}), bf16[512,2048]{0,1:T(8,128)(2,1)}) %all-gather.2.cloned.1.call-update) | async-done | bytes 2097168 | tf_op jit(solution)/shard_map/all_gather | solution.py:100
  299.4 4.5 fusion.36
  303.9 5.2 all-to-all-start
  309.1 2.9 reshape.135
  312.2 5.0 sort.17
  317.3 4.3 all-to-all-done
  323.9 6.1 gather_fusion
  330.0 63.2 %all_to_all.42 = bf16[4,8,40,2048]{3,2,1,0:T(8,128)(2,1)S(1)} all-to-all(bf16[4,8,40,2048]{3,2,1,0:T(8,128)(2,1)} %bitcast.114), channel_id=1, replica_groups=mesh['ctx'=4,'exp'=8] {'ctx'}, dimensions={0} | all-to-all | bytes 10485760 | tf_op jit(solution)/shard_map/all_to_all | solution.py:118
  394.1 120.0 %all_to_all.43 = bf16[4,8,40,2048]{3,2,0,1:T(8,128)(2,1)S(1)} all-to-all(bf16[4,8,40,2048]{3,2,0,1:T(8,128)(2,1)S(1)} %copy.174), channel_id=1, replica_groups=mesh['ctx'=4,'exp'=8] {'exp'}, dimensions={1} | all-to-all | bytes 10485760 | tf_op jit(solution)/shard_map/all_to_all | solution.py:117
  516.3 5.7 convolution_bitcast_fusion
  522.0 3.2 convolution_convert_fusion
  525.2 63.1 %all_to_all.44 = bf16[4,8,40,2048]{3,2,1,0:T(8,128)(2,1)S(1)} all-to-all(bf16[4,8,40,2048]{3,2,1,0:T(8,128)(2,1)S(1)} %bitcast.120), channel_id=1, replica_groups=mesh['ctx'=4,'exp'=8] {'ctx'}, dimensions={0} | all-to-all | bytes 10485760 | tf_op jit(solution)/shard_map/all_to_all | solution.py:139
  591.1 4.8 all-to-all-start.4
  596.0 5.2 scatter_custom_fusion
  606.8 104.2 %all-to-all-done.4 = bf16[4,8,40,2048]{3,2,0,1:T(8,128)(2,1)} async-done(((bf16[4,8,40,2048]{3,2,0,1:T(8,128)(2,1)}), bf16[4,8,40,2048]{3,2,0,1:T(8,128)(2,1)}, u32[]{:S(2)}, u32[]{:S(2)}) %all-to-all-start.4) | async-done | bytes 5242912 | tf_op jit(solution)/shard_map/all_to_all | solution.py:138
  711.0 5.7 copy.177
  716.7 14.3 %gather_fusion.1 = bf16[1280,2048]{1,0:T(8,128)(2,1)} fusion(bf16[1280,2048]{1,0:T(8,128)(2,1)} %bitcast.111, s32[2048]{0:T(1024)S(1)} %pad_clamp_fusion), kind=kCustom, calls=%fused_computation.1 | custom fusion | bytes 10490880 | tf_op jit(solution)/shard_map/gather | solution.py:150
  731.0 9.6 %reshape.130 = bf16[128,10,2048]{2,1,0:T(8,128)(2,1)} reshape(bf16[1280,2048]{1,0:T(8,128)(2,1)} %gather_fusion.1) | data formatting | bytes 10485760 | tf_op jit(solution)/shard_map/reshape | solution.py:150
  740.5 4.8 fusion.37
  (110 shorter events, 51.2 us)
Async XLA Ops:
  7.2 514.8 %copy-start = (bf16[1,512,2048]{2,1,0:T(8,128)(2,1)S(1)}, bf16[1,512,2048]{2,1,0:T(8,128)(2,1)}, u32[]{:S(2)}) copy-start(bf16[1,512,2048]{2,1,0:T(8,128)(2,1)} %param.31) | copy-start | bytes 6291460
  7.2 1.9 copy-start.15
  7.2 292.2 %all-gather.2.cloned.1.call-start = ((), (), s32[]{:S(2)}) async-start(), calls=%async_computation.5 | async-start | bytes 2621440 | tf_op jit(solution)/shard_map/all_gather | solution.py:100
  8.8 0.7 copy-start.18
  9.1 7.8 %copy-start.9 = (f32[128,8,128]{2,0,1:T(8,128)}, f32[128,8,128]{2,0,1:T(8,128)S(1)}, u32[]{:S(2)}) copy-start(f32[128,8,128]{2,0,1:T(8,128)S(1)} %copy.159) | copy-start | bytes 1572868
  9.2 5.2 copy-start.16
  17.2 1.0 copy-start.7
  182.7 2.8 copy-start.12
  182.7 2.8 copy-start.14
  187.5 5.2 copy-start.2
  187.5 2.9 copy-start.8
  194.1 4.5 copy-start.3
  194.1 4.5 copy-start.6
  207.6 4.9 collective-permute-start
  212.5 1.0 copy-start.1
  218.6 16.3 %collective-permute-start = (f32[16,128,128]{2,1,0:T(8,128)}, f32[16,128,128]{2,1,0:T(8,128)S(1)}, u32[]{:S(2)}, u32[]{:S(2)}) collective-permute-start(f32[16,128,128]{2,1,0:T(8,128)} %convolution_add_fusion.3), channel_id=1, source_target_pairs={{0,8},{8,16},{16,24},{1,9},{9,17},{17,25},{2,10},{10,18},{18,26},{... | collective-permute-start | bytes 3145736 | tf_op jit(solution)/shard_map/while/body/eval_jaxpr/ppermute | solution.py:18
  234.9 1.0 copy-start.1
  241.0 16.3 %collective-permute-start = (f32[16,128,128]{2,1,0:T(8,128)}, f32[16,128,128]{2,1,0:T(8,128)S(1)}, u32[]{:S(2)}, u32[]{:S(2)}) collective-permute-start(f32[16,128,128]{2,1,0:T(8,128)} %convolution_add_fusion.3), channel_id=1, source_target_pairs={{0,8},{8,16},{16,24},{1,9},{9,17},{17,25},{2,10},{10,18},{18,26},{... | collective-permute-start | bytes 3145736 | tf_op jit(solution)/shard_map/while/body/eval_jaxpr/ppermute | solution.py:18
  257.3 1.0 copy-start.1
  259.8 3.5 copy-start.13
  259.9 3.5 copy-start.21
  303.9 8.1 %copy-start.19 = (s32[1,128,10]{1,0,2:T(1,128)S(1)}, s32[1,128,10]{1,0,2:T(1,128)}, u32[]{:S(2)}) copy-start(s32[1,128,10]{1,0,2:T(1,128)} %param.28) | copy-start | bytes 15364
  303.9 17.8 %all-to-all-start = ((f32[4,128,512]{2,1,0:T(8,128)}), f32[4,128,512]{2,1,0:T(8,128)S(1)}, u32[]{:S(2)}, u32[]{:S(2)}) async-start(f32[4,128,512]{2,1,0:T(8,128)} %bitcast.129), calls=%async_computation | async-start | bytes 2097152 | tf_op jit(solution)/shard_map/all_to_all | solution.py:104
  309.1 14.7 %copy-start.17 = (f32[2048]{0:T(1024)S(1)}, f32[2048]{0:T(1024)}, u32[]{:S(2)}) copy-start(f32[2048]{0:T(1024)} %param.27) | copy-start | bytes 24580
  321.7 2.1 copy-start.4
  321.7 1.6 copy-start.11
  321.7 2.1 copy-start.10
  514.1 2.2 copy-start.22
  591.0 4.8 copy-start.20
  591.1 10.2 %copy-start.5 = (f32[4,128,512]{2,1,0:T(8,128)S(1)}, f32[4,128,512]{2,1,0:T(8,128)}, u32[]{:S(2)}) copy-start(f32[4,128,512]{2,1,0:T(8,128)} %copy-done.4) | copy-start | bytes 3145732
  591.1 120.0 %all-to-all-start.4 = ((bf16[4,8,40,2048]{3,2,0,1:T(8,128)(2,1)}), bf16[4,8,40,2048]{3,2,0,1:T(8,128)(2,1)}, u32[]{:S(2)}, u32[]{:S(2)}) async-start(bf16[4,8,40,2048]{3,2,0,1:T(8,128)(2,1)} %copy.176), calls=%async_computation.4 | async-start | bytes 10485760 | tf_op jit(solution)/shard_map/all_to_all | solution.py:138
Sparse Core Ops, SparseCore 0:
  264.7 34.6 all-gather.1
where the time goes:
time: 763 us; the launch traced here: 754 us
  blocking collectives  246 us (32%)
  other arithmetic  179 us (23%)
  waiting for transfers between devices  177 us (23%)
  local copies, waits for them, and re-layouts  69.3 us (9%)
  matrix products  53.1 us (7%)
  between operations  15 us (2%)
  starting transfers between devices  13.8 us (2%)
    another operation x3, other arithmetic, on_device(): jax.scipy.linalg.solve_triangular(unit_lower, right_side, lower=True, uni...  159 us
    all_to_all x1, blocking collectives, on_device(): lax.all_to_all(lax.all_to_all(outgoing, 'ctx', split_axis=0, concat_axis=...  120 us
    all_to_all x1, waiting for transfers between devices, on_device(): lax.all_to_all(lax.all_to_all(produced, 'ctx', split_axis=0, concat_axis=...  104 us
    all_to_all x1, blocking collectives, on_device(): lax.all_to_all(outgoing, 'ctx', split_axis=0, concat_axis=0, tiled=True)  63.2 us
    all_to_all x1, blocking collectives, on_device(): lax.all_to_all(produced, 'ctx', split_axis=0, concat_axis=0, tiled=True)  63.1 us
    all_gather x1, waiting for transfers between devices, on_device(): lax.all_gather(gated, 'ctx', axis=0, tiled=True)  34.8 us
    ppermute x3, waiting for transfers between devices, shifted(): lax.ppermute(value, axis, [(source, source + steps) for source in range(f...  33.7 us
  transfers between devices with their start and end apart: 6, of which 6 were waited for; matrix products, arithmetic and copies ran while one was open for 2% of the time, Pallas kernels for 0%

commit v1 on v0

--- a/solution.py
+++ b/solution.py
@@ -1,6 +1,10 @@
+import functools
+
 import jax
 import jax.numpy as jnp
 from jax import lax
+from jax.experimental import pallas as pl
+from jax.experimental.pallas import tpu as pltpu
 from jax.sharding import PartitionSpec as P
 
 D = 2048
@@ -16,6 +20,313 @@
     count = lax.axis_size(axis)
     first, last = (max(0, -steps), min(count, count - steps))
     return lax.ppermute(value, axis, [(source, source + steps) for source in range(first, last)])
+
+
+BF = jnp.bfloat16
+MESH = pl.DeviceIdType.MESH
+BASE = 16
+
+
+def mm(a, b):
+    return lax.dot_general(
+        a.astype(BF), b.astype(BF), (((1,), (0,)), ((), ())), preferred_element_type=jnp.float32
+    )
+
+
+def mm_nt(a, b):
+    return lax.dot_general(
+        a.astype(BF), b.astype(BF), (((1,), (1,)), ((), ())), preferred_element_type=jnp.float32
+    )
+
+
+def mm_tn(a, b):
+    return lax.dot_general(
+        a.astype(BF), b.astype(BF), (((0,), (0,)), ((), ())), preferred_element_type=jnp.float32
+    )
+
+
+def unit_lower_inverse(lowers, rows, cols, eye):
+    length = rows.shape[0]
+    same = (rows // BASE) == (cols // BASE)
+    powers = [jnp.where(same, -low, 0.0) for low in lowers]
+    xs = [eye + p for p in powers]
+    span = 2
+    while span < BASE:
+        powers = [mm(p, p) for p in powers]
+        xs = [x + mm(x, p) for x, p in zip(xs, powers)]
+        span *= 2
+    size = BASE
+    while size < length:
+        inside = ((rows // (2 * size)) == (cols // (2 * size))) & ((rows // size) > (cols // size))
+        mids = [mm(jnp.where(inside, low, 0.0), x) for low, x in zip(lowers, xs)]
+        xs = [x - mm(x, m) for x, m in zip(xs, mids)]
+        size *= 2
+    return xs
+
+
+def delta_head(query, keys, values, rate_rows, cum_rows):
+    length = query.shape[0]
+    rows = lax.broadcasted_iota(jnp.int32, (length, length), 0)
+    cols = lax.broadcasted_iota(jnp.int32, (length, length), 1)
+    diag = rows == cols
+    eye = jnp.where(diag, 1.0, 0.0)
+    query = query.astype(jnp.float32)
+    key = keys.astype(jnp.float32)
+    key = key * lax.rsqrt(jnp.sum(key * key, axis=-1, keepdims=True) + 1e-06)
+    kk = mm_nt(key, key)
+    qk = mm_nt(query, key)
+    column = lambda row: jnp.sum(jnp.where(diag, row, 0.0), axis=1, keepdims=True)
+    lowers, parts = [], []
+    for value, rate_row, cum_row in zip(values, rate_rows, cum_rows):
+        cum, rate = column(cum_row), column(rate_row)
+        last = cum_row[:, length - 1 :]
+        spread = jnp.exp(jnp.where(rows >= cols, cum - cum_row, 0.0))
+        lowers.append(jnp.where(rows > cols, rate * spread * kk, 0.0))
+        parts.append((value.astype(jnp.float32), cum, rate, last, spread))
+    inverses = unit_lower_inverse(lowers, rows, cols, eye)
+    results = []
+    for inverse, (value, cum, rate, last, spread) in zip(inverses, parts):
+        now = jnp.exp(cum)
+        solved = mm(inverse, jnp.concatenate([rate * value, (rate * now) * key], axis=1))
+        attend = jnp.where(rows >= cols, spread * qk, 0.0)
+        inner = mm(attend, solved)
+        tail = mm_tn(jnp.exp(last - cum) * key, solved)
+        dv = value.shape[1]
+        results.append(
+            (
+                inner[:, :dv],
+                now * query - inner[:, dv:],
+                jnp.exp(last) * eye - tail[:, dv:],
+                tail[:, :dv],
+            )
+        )
+    return results
+
+
+def delta_kernel(group, q_ref, k_ref, v_ref, rate_ref, cum_ref, intra_ref, qeff_ref, trans_ref, add_ref):
+    width = v_ref.shape[1] // group
+    results = delta_head(
+        q_ref[...],
+        k_ref[...],
+        [v_ref[:, i * width : (i + 1) * width] for i in range(group)],
+        [rate_ref[0, i : i + 1, :] for i in range(group)],
+        [cum_ref[0, i : i + 1, :] for i in range(group)],
+    )
+    for i, (intra, qeff, trans, add) in enumerate(results):
+        intra_ref[i] = intra
+        qeff_ref[i] = qeff.astype(qeff_ref.dtype)
+        trans_ref[i] = trans
+        add_ref[i] = add
+
+
+def delta_local(query, key, value, rate, cum):
+    length = query.shape[0]
+    heads = rate.shape[0]
+    group = heads // HK
+    out = jax.ShapeDtypeStruct((heads, length, DV), jnp.float32)
+    outb = jax.ShapeDtypeStruct((heads, length, DK), BF)
+    sq = jax.ShapeDtypeStruct((heads, DK, DK), jnp.float32)
+    sv = jax.ShapeDtypeStruct((heads, DK, DV), jnp.float32)
+    block = lambda a, b: pl.BlockSpec((group, a, b), lambda h: (h, 0, 0))
+    rows = pl.BlockSpec((1, group, length), lambda h: (h, 0, 0))
+    return pl.pallas_call(
+        functools.partial(delta_kernel, group),
+        out_shape=(out, outb, sq, sv),
+        grid=(HK,),
+        in_specs=[
+            pl.BlockSpec((length, DK), lambda h: (0, h)),
+            pl.BlockSpec((length, DK), lambda h: (0, h)),
+            pl.BlockSpec((length, group * DV), lambda h: (0, h)),
+            rows,
+            rows,
+        ],
+        out_specs=(block(length, DV), block(length, DK), block(DK, DK), block(DK, DV)),
+        cost_estimate=pl.CostEstimate(flops=20 * heads * 2 * length**3, bytes_accessed=8 << 20, transcendentals=heads * length * length),
+    )(query, key, value, rate.reshape(HK, group, length), cum.reshape(HK, group, length))
+
+
+def moe_kernel(
+    planes, lanes_x, tok_ref, pick_ref, up_ref, down_ref, out_ref,
+    tokbuf, pickbuf, sendbuf, recvbuf, prodbuf, retbuf, partbuf, zbuf, total,
+    tok_send, tok_recv, pick_send, pick_recv, d_send, d_recv, r_send, r_recv, z_send, z_recv,
+):
+    c = lax.axis_index("ctx")
+    e = lax.axis_index("exp")
+    z = e // lanes_x
+    x = e % lanes_x
+    ctx = lax.axis_size("ctx")
+    peers = ctx * lanes_x
+    mine = c * lanes_x + x
+    slots = sendbuf.shape[2]
+    width = tok_ref.shape[1]
+    ff = down_ref.shape[0]
+
+    def plane_device(q):
+        return (q // lanes_x, z * lanes_x + q % lanes_x)
+
+    def line_device(zz):
+        return (c, zz * lanes_x + x)
+
+    barrier = pltpu.get_barrier_semaphore()
+    for d in range(1, peers):
+        pl.semaphore_signal(barrier, inc=1, device_id=plane_device((mine + d) % peers), device_id_type=MESH)
+    for d in range(1, planes):
+        pl.semaphore_signal(barrier, inc=1, device_id=line_device((z + d) % planes), device_id_type=MESH)
+    pl.semaphore_wait(barrier, peers + planes - 2)
+
+    def remote(src, dst, ssem, rsem, device):
+        return pltpu.make_async_remote_copy(
+            src_ref=src, dst_ref=dst, send_sem=ssem, recv_sem=rsem, device_id=device, device_id_type=MESH
+        )
+
+    def step_of(i):
+        return (i % 2) * ((i + 1) // 2) + (1 - i % 2) * ((planes - i // 2) % planes)
+
+    def tok_copy(s):
+        return remote(tok_ref, tokbuf.at[s], tok_send.at[s], tok_recv.at[s], line_device((z + s) % planes))
+
+    def pick_copy(s):
+        there = (z + s) % planes
+        return remote(pick_ref.at[there], pickbuf.at[s], pick_send.at[s], pick_recv.at[s], line_device(there))
+
+    def d_copy(s, q):
+        return remote(sendbuf.at[s, q], recvbuf.at[s, mine], d_send.at[s, q], d_recv.at[s, mine], plane_device(q))
+
+    def d_arrival(s, q):
+        return remote(sendbuf.at[s, q], recvbuf.at[s, q], d_send.at[s, q], d_recv.at[s, q], plane_device(q))
+
+    def r_copy(s, q):
+        return remote(prodbuf.at[s, q], retbuf.at[s, mine], r_send.at[s, q], r_recv.at[s, mine], plane_device(q))
+
+    def r_arrival(s, q):
+        return remote(prodbuf.at[s, q], retbuf.at[s, q], r_send.at[s, q], r_recv.at[s, q], plane_device(q))
+
+    def z_copy(s):
+        return remote(partbuf.at[s], zbuf.at[s], z_send.at[s], z_recv.at[s], line_device((z - s + planes) % planes))
+
+    for i in range(1, planes):
+        s = (i + 1) // 2 if i % 2 else (planes - i // 2) % planes
+        pick_copy(s).start()
+        tok_copy(s).start()
+    tokbuf[0] = tok_ref[...]
+    pickbuf[0] = pick_ref[z]
+
+    def body(i, carry):
+        @pl.when(i < planes)
+        def _():
+            s = step_of(i)
+
+            @pl.when(i > 0)
+            def _():
+                pick_copy(s).wait_recv()
+                tok_copy(s).wait_recv()
+
+            chosen = jnp.where(pickbuf[s].astype(jnp.float32) != 0.0, 1.0, 0.0).astype(BF)
+            rows = mm(chosen, tokbuf[s])
+            sendbuf[s] = rows.reshape(peers, slots, width).astype(BF)
+            for d in range(1, peers):
+                d_copy(s, (mine + d) % peers).start()
+            recvbuf[s, mine] = sendbuf[s, mine]
+
+        @pl.when((i >= 1) & (i < planes + 1))
+        def _():
+            s = step_of(i - 1)
+            for d in range(1, peers):
+                d_arrival(s, (mine + d) % peers).wait_recv()
+            rows = recvbuf[s].astype(jnp.float32).reshape(peers * slots, width).astype(BF)
+            gate = mm(rows, up_ref[:, :ff])
+            hidden = (gate / (1.0 + jnp.exp(-gate)) * mm(rows, up_ref[:, ff:])).astype(BF)
+            made = mm(hidden, down_ref[...])
+            prodbuf[s] = made.reshape(peers, slots, width).astype(BF)
+            for d in range(1, peers):
+                r_copy(s, (mine + d) % peers).start()
+            retbuf[s, mine] = prodbuf[s, mine]
+
+        @pl.when(i >= 2)
+        def _():
+            s = step_of(i - 2)
+            for d in range(1, peers):
+                r_arrival(s, (mine + d) % peers).wait_recv()
+            rows = retbuf[s].astype(jnp.float32).reshape(peers * slots, width).astype(BF)
+            part = mm_tn(pickbuf[s], rows)
+
+            @pl.when(i == 2)
+            def _():
+                total[...] = part
+
+            @pl.when(i > 2)
+            def _():
+                partbuf[s] = part.astype(BF)
+                z_copy(s).start()
+
+        return carry
+
+    lax.fori_loop(0, planes + 2, body, 0)
+
+    for s in range(1, planes):
+        z_copy(s).wait_recv()
+        total[...] += zbuf[s].astype(jnp.float32)
+    out_ref[...] = total[...].astype(out_ref.dtype)
+
+    for s in range(1, planes):
+        tok_copy(s).wait_send()
+        pick_copy(s).wait_send()
+        z_copy(s).wait_send()
+
+    def drain(s, carry):
+        for d in range(1, peers):
+            d_copy(s, (mine + d) % peers).wait_send()
+            r_copy(s, (mine + d) % peers).wait_send()
+        return carry
+
+    lax.fori_loop(0, planes, drain, 0)
+
+
+def moe_planes(moe_in, routes, route_gate, expert_up, expert_down, planes, lanes_x):
+    length, width = moe_in.shape
+    ctx = lax.axis_size("ctx")
+    peers = ctx * lanes_x
+    experts = peers * planes
+    slots = length * TOP // experts
+    ids = jnp.arange(experts, dtype=jnp.int32)
+    hit = routes[:, :, None] == ids
+    named = jnp.any(hit, axis=1)
+    weight = jnp.sum(jnp.where(hit, route_gate[:, :, None], 0.0), axis=1).T
+    ones = named.astype(BF)
+    before = (
+        lax.broadcasted_iota(jnp.int32, (length, length), 0)
+        < lax.broadcasted_iota(jnp.int32, (length, length), 1)
+    ).astype(BF)
+    rank = lax.dot_general(ones, before, (((0,), (0,)), ((), ())), preferred_element_type=jnp.float32)
+    rank = jnp.where(named.T, rank, -1.0)
+
+    def by_plane(v):
+        return v.reshape(ctx, planes, lanes_x, length).transpose(1, 0, 2, 3)
+
+    slot = jnp.arange(slots, dtype=jnp.float32)[None, None, None, :, None]
+    pick = jnp.where(by_plane(rank)[:, :, :, None, :] == slot, by_plane(weight)[:, :, :, None, :], 0.0)
+    pick = pick.astype(BF).reshape(planes, peers * slots, length)
+    dma = pltpu.SemaphoreType.DMA
+    rows_shape = pltpu.VMEM((planes, peers, slots, width), BF)
+    block = pltpu.VMEM((planes, length, width), BF)
+    return pl.pallas_call(
+        functools.partial(moe_kernel, planes, lanes_x),
+        out_shape=jax.ShapeDtypeStruct((length, width), BF),
+        in_specs=[pl.BlockSpec(memory_space=pltpu.VMEM)] * 4,
+        out_specs=pl.BlockSpec(memory_space=pltpu.VMEM),
+        scratch_shapes=[
+            block,
+            pltpu.VMEM((planes, peers * slots, length), BF),
+            rows_shape, rows_shape, rows_shape, rows_shape,
+            block,
+            block,
+            pltpu.VMEM((length, width), jnp.float32),
+            dma((planes,)), dma((planes,)), dma((planes,)), dma((planes,)),
+            dma((planes, peers)), dma((planes, peers)), dma((planes, peers)), dma((planes, peers)),
+            dma((planes,)), dma((planes,)),
+        ],
+        compiler_params=pltpu.CompilerParams(collective_id=1, has_side_effects=True, vmem_limit_bytes=60 << 20),
+    )(moe_in, pick, expert_up[0], expert_down[0])
 
 
 def on_device(
@@ -37,49 +348,10 @@
 ):
     highest = lax.Precision.HIGHEST
     length = stream.shape[1]
-    repeat = OUTPUT_CHANNELS // HK
-    query_loc = jnp.repeat(
-        queries[0].astype(jnp.float32).reshape(length, HK, DK), repeat, axis=1
-    ).transpose(1, 0, 2)
-    key_loc = key_proj[0].astype(jnp.float32).reshape(length, HK, DK)
-    key_loc = key_loc * lax.rsqrt(jnp.sum(key_loc * key_loc, axis=-1, keepdims=True) + 1e-06)
-    key_loc = jnp.repeat(key_loc, repeat, axis=1).transpose(1, 0, 2)
-    value_loc = (
-        value_proj[0].astype(jnp.float32).reshape(length, OUTPUT_CHANNELS, DV).transpose(1, 0, 2)
-    )
-    rate_loc = write_rate[0].T
     cumulative = jnp.cumsum(log_decay[0], axis=0).T
-    later = lax.broadcasted_iota(jnp.int32, (length, length), 0)
-    earlier = lax.broadcasted_iota(jnp.int32, (length, length), 1)
-    strict = later > earlier
-    inclusive = later >= earlier
-    spread = jnp.exp(
-        jnp.where(inclusive[None], cumulative[:, :, None] - cumulative[:, None, :], 0.0)
-    )
-    key_key = jnp.einsum("htd,hsd->hts", key_loc, key_loc, precision=highest)
-    query_key = jnp.einsum("htd,hsd->hts", query_loc, key_loc, precision=highest)
-    lower_part = jnp.where(strict[None], rate_loc[:, :, None] * spread * key_key, 0.0)
-    attend = jnp.where(inclusive[None], spread * query_key, 0.0)
-    decay_now = jnp.exp(cumulative)
-    right_side = jnp.concatenate(
-        [rate_loc[:, :, None] * value_loc, (rate_loc * decay_now)[:, :, None] * key_loc], axis=-1
-    )
-    unit_lower = jnp.eye(length, dtype=jnp.float32)[None] + lower_part
-    solved = jax.scipy.linalg.solve_triangular(
-        unit_lower, right_side, lower=True, unit_diagonal=True
-    )
-    update = solved[:, :, :DV]
-    w_rows = solved[:, :, DV:]
-    intra = jnp.einsum("hts,hsv->htv", attend, update, precision=highest)
-    query_eff = decay_now[:, :, None] * query_loc - jnp.einsum(
-        "hts,hsd->htd", attend, w_rows, precision=highest
-    )
-    key_tail = jnp.exp(cumulative[:, -1:] - cumulative)[:, :, None] * key_loc
-    eye_key = jnp.eye(DK, dtype=jnp.float32)[None]
-    transit = decay_now[:, -1][:, None, None] * eye_key - jnp.einsum(
-        "htd,hte->hde", key_tail, w_rows, precision=highest
-    )
-    carry_add = jnp.einsum("htd,htv->hdv", key_tail, update, precision=highest)
+    intra, query_eff, transit, carry_add = delta_local(
+        queries[0], key_proj[0], value_proj[0], write_rate[0].T, cumulative
+    )
     first_state = init_state[0]
     position = lax.axis_index("ctx")
 
@@ -89,7 +361,9 @@
         return jnp.where(position == 0, first_state, incoming)
 
     start_state = lax.fori_loop(0, lax.axis_size("ctx") - 1, relay_step, first_state)
-    head_out = intra + jnp.einsum("htd,hdv->htv", query_eff, start_state, precision=highest)
+    head_out = intra + jnp.einsum(
+        "htd,hdv->htv", query_eff, start_state.astype(BF), preferred_element_type=jnp.float32
+    )
     gate_loc = (
         gate_proj[0].astype(jnp.float32).reshape(length, OUTPUT_CHANNELS, DV).transpose(1, 0, 2)
     )
@@ -110,6 +384,13 @@
     ctx_count = lax.axis_size("ctx")
     exp_count = lax.axis_size("exp")
     local_experts = expert_up.shape[0]
+    lanes_x = max(1, ctx_count // 2)
+    even = exp_count % lanes_x == 0 and length * TOP % (8 * ctx_count * exp_count) == 0
+    if local_experts == 1 and even:
+        moe_output = moe_planes(
+            moe_in, routes[0], route_gate[0], expert_up, expert_down, exp_count // lanes_x, lanes_x
+        )
+        return (mixed[None], moe_output[None])
     flat_routes = routes[0].reshape(-1)
     order = jnp.argsort(flat_routes, stable=True)
     per_owner = length * TOP // (ctx_count * exp_count)

time: 763 us -> 324 us (0.42)
  blocking collectives: 246 us -> 0 us
  Pallas kernels: 0 us -> 171 us
  other arithmetic: 179 us -> 12.3 us
  waiting for transfers between devices: 177 us -> 76.9 us
  local copies, waits for them, and re-layouts: 69.3 us -> 20.7 us
  matrix products: 53.1 us -> 17.8 us
    all_to_all x3 -> x0, blocking collectives: 246 us -> none  [the longest x1 120 us: on_device(): lax.all_to_all(lax.all_to_all(outgoing, 'ctx', split_axis=0, concat_axis=...]
    pallas_call x0 -> x2, Pallas kernels: none -> 171 us  [the longest x1 151 us: moe_planes(): pl.pallas_call(functools.partial(moe_kernel, planes, lanes_x), out_shape=...]
    another operation x3 -> x0, other arithmetic: 159 us -> none  [on_device(): jax.scipy.linalg.solve_triangular(unit_lower, right_side, lower=True, uni...]
    all_to_all x1 -> x0, waiting for transfers between devices: 104 us -> none  [on_device(): lax.all_to_all(lax.all_to_all(produced, 'ctx', split_axis=0, concat_axis=...]
    dot_general x10 -> x2, matrix products: 35.5 us -> 2.89 us  [the longest x1 2.76 us: on_device(): jnp.einsum('htd,hdv->htv', query_eff, start_state.astype(BF), preferred_e...]
    gather x2 -> x0, local copies, waits for them, and re-layouts: 20.4 us -> none  [the longest x1 14.3 us: on_device(): returned.reshape(length * TOP, D)[inverse].reshape(length, TOP, D)]
    all_to_all x4 -> x0, local copies, waits for them, and re-layouts: 10.2 us -> none  [the longest x1 5.67 us: on_device(): lax.all_to_all(lax.all_to_all(produced, 'ctx', split_axis=0, concat_axis=...]
    reshape x1 -> x0, local copies, waits for them, and re-layouts: 9.56 us -> none  [on_device(): returned.reshape(length * TOP, D)[inverse].reshape(length, TOP, D)]
  transfers between devices with their start and end apart: 6 -> 5, of which waited for: 6 -> 5; matrix products, arithmetic and copies ran while one was open for 2% -> 1% of each run, Pallas kernels for 0% -> 0%
where the time goes in v1:
time: 324 us; the launch traced here: 322 us
  Pallas kernels  171 us (53%)
  waiting for transfers between devices  76.9 us (24%)
  local copies, waits for them, and re-layouts  20.7 us (6%)
  matrix products  17.8 us (5%)
  between operations  14.1 us (4%)
  other arithmetic  12.3 us (4%)
  starting transfers between devices  9.05 us (3%)
    pallas_call x1, Pallas kernels, moe_planes(): pl.pallas_call(functools.partial(moe_kernel, planes, lanes_x), out_shape=...  151 us
    all_gather x1, waiting for transfers between devices, on_device(): lax.all_gather(gated, 'ctx', axis=0, tiled=True)  34.8 us
    ppermute x3, waiting for transfers between devices, shifted(): lax.ppermute(value, axis, [(source, source + steps) for source in range(f...  33.7 us
    pallas_call x1, Pallas kernels, delta_local(): pl.pallas_call(functools.partial(delta_kernel, group), out_shape=(out, ou...  20.1 us
    dot_general x3, matrix products, relay_step(): jnp.einsum('hde,hev->hdv', transit, start_state, precision=highest)  11 us
    all_to_all x1, waiting for transfers between devices, on_device(): lax.all_to_all(column_block, 'ctx', split_axis=0, concat_axis=1, tiled=True)  8.39 us
  transfers between devices with their start and end apart: 5, of which 5 were waited for; matrix products, arithmetic and copies ran while one was open for 1% of the time, Pallas kernels for 0%

profile of v1, /device:TPU:5, one launch (start us, length us, event | category | flops | bytes accessed | tf_op | source)
XLA Modules:
  0.0 322.3 jit_solution(9115377177037334573)
XLA Ops:
  9.0 1.2 copy.82
  10.2 20.1 %shard_map.158 = (f32[16,128,128]{2,1,0:T(8,128)}, bf16[16,128,128]{2,1,0:T(8,128)(2,1)}, f32[16,128,128]{2,1,0:T(8,128)}, f32[16,128,128]{2,1,0:T(8,128)}) custom-call(bf16[128,1024]{1,0:T(8,128)(2,1)} %bitcast.102, bf16[128,1024]{1,0:T(8,128)(2,1)} %bitcast.103, bf16[128,2048]{1,0:T(8,128)(2,1)} %bitcast.101, f32[8,2,128]{2,1,0:T(2,128)} %bitcast.104, ...), custom_call_target="tpu_custom_call" | custom-call | flops 1342177280 | bytes 8388608 | tf_op jit(solution)/shard_map/pallas_call | solution.py:132
  30.3 55.6 %while.12 = (s32[]{:T(128)}, f32[16,128,128]{2,1,0:T(8,128)S(1)}, pred[]{:T(512)}, f32[16,128,128]{2,1,0:T(8,128)}, f32[16,128,128]{2,1,0:T(8,128)}, /*index=5*/f32[16,128,128]{2,1,0:T(8,128)}, s32[]{:T(128)}) while((s32[]{:T(128)}, f32[16,128,128]{2,1,0:T(8,128)S(1)}, pred[]{:T(512)}, f32[16,128,128]{2,1,0:T(8,128)}, ...), condition=%wide.region_2.3_spmd, body=%wide.region_1.2_spmd.sunk | while | flops 403177472 | bytes 15728786 | solution.py:363
  30.3 3.7 %convolution_add_fusion.3 = f32[16,128,128]{2,1,0:T(8,128)} fusion(f32[16,128,128]{2,1,0:T(8,128)} %get-tuple-element.152, f32[16,128,128]{2,1,0:T(8,128)} %get-tuple-element.151, f32[16,128,128]{2,1,0:T(8,128)S(1)} %get-tuple-element.142), kind=kOutput, calls=%fused_computation.clone.1 | convolution fusion | flops 402915328 | bytes 4194304 | tf_op jit(solution)/shard_map/while/body/eval_jaxpr/hde,hev->hdv/dot_general | solution.py:359
  34.0 1.3 collective-permute-start
  35.3 3.6 %collective-permute-done = f32[16,128,128]{2,1,0:T(8,128)S(1)} collective-permute-done((f32[16,128,128]{2,1,0:T(8,128)}, f32[16,128,128]{2,1,0:T(8,128)S(1)}, u32[]{:S(2)}, u32[]{:S(2)}) %collective-permute-start) | collective-permute-done | bytes 1048608 | tf_op jit(solution)/shard_map/while/body/eval_jaxpr/ppermute | solution.py:22
  38.9 1.0 copy-done.1
  39.9 1.3 broadcast_select_fusion.2
  41.3 3.7 %convolution_add_fusion.3 = f32[16,128,128]{2,1,0:T(8,128)} fusion(f32[16,128,128]{2,1,0:T(8,128)} %get-tuple-element.152, f32[16,128,128]{2,1,0:T(8,128)} %get-tuple-element.151, f32[16,128,128]{2,1,0:T(8,128)S(1)} %get-tuple-element.142), kind=kOutput, calls=%fused_computation.clone.1 | convolution fusion | flops 402915328 | bytes 4194304 | tf_op jit(solution)/shard_map/while/body/eval_jaxpr/hde,hev->hdv/dot_general | solution.py:359
  44.9 1.3 collective-permute-start
  46.2 15.0 %collective-permute-done = f32[16,128,128]{2,1,0:T(8,128)S(1)} collective-permute-done((f32[16,128,128]{2,1,0:T(8,128)}, f32[16,128,128]{2,1,0:T(8,128)S(1)}, u32[]{:S(2)}, u32[]{:S(2)}) %collective-permute-start) | collective-permute-done | bytes 1048608 | tf_op jit(solution)/shard_map/while/body/eval_jaxpr/ppermute | solution.py:22
  61.3 1.0 copy-done.1
  62.2 1.3 broadcast_select_fusion.2
  63.6 3.7 %convolution_add_fusion.3 = f32[16,128,128]{2,1,0:T(8,128)} fusion(f32[16,128,128]{2,1,0:T(8,128)} %get-tuple-element.152, f32[16,128,128]{2,1,0:T(8,128)} %get-tuple-element.151, f32[16,128,128]{2,1,0:T(8,128)S(1)} %get-tuple-element.142), kind=kOutput, calls=%fused_computation.clone.1 | convolution fusion | flops 402915328 | bytes 4194304 | tf_op jit(solution)/shard_map/while/body/eval_jaxpr/hde,hev->hdv/dot_general | solution.py:359
  67.3 1.3 collective-permute-start
  68.6 15.0 %collective-permute-done = f32[16,128,128]{2,1,0:T(8,128)S(1)} collective-permute-done((f32[16,128,128]{2,1,0:T(8,128)}, f32[16,128,128]{2,1,0:T(8,128)S(1)}, u32[]{:S(2)}, u32[]{:S(2)}) %collective-permute-start) | collective-permute-done | bytes 1048608 | tf_op jit(solution)/shard_map/while/body/eval_jaxpr/ppermute | solution.py:22
  84.6 1.3 broadcast_select_fusion.2
  85.9 2.8 multiply_reduce_fusion.1
  88.7 2.1 copy.55
  90.8 2.2 copy.56
  93.0 2.4 fusion.9
  95.5 2.0 copy.57
  97.5 34.8 %all-gather.2.cloned.1.call-done = bf16[512,2048]{0,1:T(8,128)(2,1)} async-done(((bf16[128,2048]{0,1:T(8,128)(2,1)}), bf16[512,2048]{0,1:T(8,128)(2,1)}) %all-gather.2.cloned.1.call-update) | async-done | bytes 2097168 | tf_op jit(solution)/shard_map/all_gather | solution.py:374
  132.4 3.9 %fusion.11 = f32[512,512]{1,0:T(8,128)} fusion(bf16[512,2048]{0,1:T(8,128)(2,1)} %all-gather.2.cloned.1.call-done, bf16[2048,512]{1,0:T(8,128)(2,1)S(1)} %copy-done), kind=kOutput, calls=%fused_computation.32 | convolution fusion | flops 1073741824 | bytes 5242880 | tf_op jit(solution)/shard_map/dot_general | solution.py:373
  136.2 5.2 %all-to-all-start = ((f32[4,128,512]{2,1,0:T(8,128)}), f32[4,128,512]{2,1,0:T(8,128)S(1)}, u32[]{:S(2)}, u32[]{:S(2)}) async-start(f32[4,128,512]{2,1,0:T(8,128)} %bitcast.92), calls=%async_computation | async-start | bytes 2097152 | tf_op jit(solution)/shard_map/all_to_all | solution.py:378
  141.4 2.8 reshape.62
  145.4 8.4 %all-to-all-done = f32[4,128,512]{2,1,0:T(8,128)S(1)} async-done(((f32[4,128,512]{2,1,0:T(8,128)}), f32[4,128,512]{2,1,0:T(8,128)S(1)}, u32[]{:S(2)}, u32[]{:S(2)}) %all-to-all-start) | async-done | bytes 1048608 | tf_op jit(solution)/shard_map/all_to_all | solution.py:378
  153.8 1.7 multiply_reduce_fusion
  156.6 151.2 %shard_map.159 = bf16[128,2048]{1,0:T(8,128)(2,1)} custom-call(bf16[128,2048]{1,0:T(8,128)(2,1)} %multiply_convert_fusion.tok_ref, bf16[4,320,128]{2,1,0:T(8,128)(2,1)} %fusion.7.pick_ref, bf16[2048,1024]{1,0:T(8,128)(2,1)} %bitcast.87, bf16[512,2048]{1,0:T(8,128)(2,1)} %bitcast.90), custom_call_target="tpu_custom_call" | custom-call | tf_op jit(solution)/shard_map/pallas_call | solution.py:312
  307.8 1.6 copy.58
  309.5 3.0 all_to_all.19
  312.5 2.1 add_convert_fusion
  (40 shorter events, 5.9 us)
Async XLA Ops:
  7.2 125.2 %copy-start = (bf16[2048,512]{1,0:T(8,128)(2,1)S(1)}, bf16[2048,512]{1,0:T(8,128)(2,1)}, u32[]{:S(2)}) copy-start(bf16[2048,512]{1,0:T(8,128)(2,1)} %param.26) | copy-start | bytes 6291460
  7.2 125.2 %all-gather.2.cloned.1.call-start = ((), (), s32[]{:S(2)}) async-start(), calls=%async_computation.1 | async-start | bytes 2621440 | tf_op jit(solution)/shard_map/all_gather | solution.py:374
  34.0 4.9 %collective-permute-start = (f32[16,128,128]{2,1,0:T(8,128)}, f32[16,128,128]{2,1,0:T(8,128)S(1)}, u32[]{:S(2)}, u32[]{:S(2)}) collective-permute-start(f32[16,128,128]{2,1,0:T(8,128)} %convolution_add_fusion.3), channel_id=1, source_target_pairs={{0,8},{8,16},{16,24},{1,9},{9,17},{17,25},{2,10},{10,18},{18,26},{... | collective-permute-start | bytes 3145736 | tf_op jit(solution)/shard_map/while/body/eval_jaxpr/ppermute | solution.py:22
  38.9 1.0 copy-start.1
  44.9 16.3 %collective-permute-start = (f32[16,128,128]{2,1,0:T(8,128)}, f32[16,128,128]{2,1,0:T(8,128)S(1)}, u32[]{:S(2)}, u32[]{:S(2)}) collective-permute-start(f32[16,128,128]{2,1,0:T(8,128)} %convolution_add_fusion.3), channel_id=1, source_target_pairs={{0,8},{8,16},{16,24},{1,9},{9,17},{17,25},{2,10},{10,18},{18,26},{... | collective-permute-start | bytes 3145736 | tf_op jit(solution)/shard_map/while/body/eval_jaxpr/ppermute | solution.py:22
  61.3 1.0 copy-start.1
  67.3 16.3 %collective-permute-start = (f32[16,128,128]{2,1,0:T(8,128)}, f32[16,128,128]{2,1,0:T(8,128)S(1)}, u32[]{:S(2)}, u32[]{:S(2)}) collective-permute-start(f32[16,128,128]{2,1,0:T(8,128)} %convolution_add_fusion.3), channel_id=1, source_target_pairs={{0,8},{8,16},{16,24},{1,9},{9,17},{17,25},{2,10},{10,18},{18,26},{... | collective-permute-start | bytes 3145736 | tf_op jit(solution)/shard_map/while/body/eval_jaxpr/ppermute | solution.py:22
  83.6 1.0 copy-start.1
  88.7 4.4 %copy-start.4 = (f32[16,128,128]{2,1,0:T(8,128)S(1)}, f32[16,128,128]{2,1,0:T(8,128)}, u32[]{:S(2)}) copy-start(f32[16,128,128]{2,1,0:T(8,128)} %get-tuple-element.96) | copy-start | bytes 3145732
  88.7 4.4 %copy-start.9 = (f32[128]{0:T(128)S(1)}, f32[128]{0:T(128)}, u32[]{:S(2)}) copy-start(f32[128]{0:T(128)} %param.25) | copy-start | bytes 1540
  136.2 8.0 %copy-start.7 = (s32[1,128,10]{1,0,2:T(1,128)S(1)}, s32[1,128,10]{1,0,2:T(1,128)}, u32[]{:S(2)}) copy-start(s32[1,128,10]{1,0,2:T(1,128)} %param.28) | copy-start | bytes 15364
  136.2 8.0 %copy-start.8 = (f32[1,128,10]{1,0,2:T(1,128)S(1)}, f32[1,128,10]{1,0,2:T(1,128)}, u32[]{:S(2)}) copy-start(f32[1,128,10]{1,0,2:T(1,128)} %param.29) | copy-start | bytes 15364
  136.2 17.6 %all-to-all-start = ((f32[4,128,512]{2,1,0:T(8,128)}), f32[4,128,512]{2,1,0:T(8,128)S(1)}, u32[]{:S(2)}, u32[]{:S(2)}) async-start(f32[4,128,512]{2,1,0:T(8,128)} %bitcast.92), calls=%async_computation | async-start | bytes 2097152 | tf_op jit(solution)/shard_map/all_to_all | solution.py:378
  145.4 10.2 %copy-start.6 = (f32[2048]{0:T(1024)S(1)}, f32[2048]{0:T(1024)}, u32[]{:S(2)}) copy-start(f32[2048]{0:T(1024)} %param.27) | copy-start | bytes 24580
  153.8 1.9 copy-start.2
  309.5 3.0 copy-start.3
  309.5 5.2 %copy-start.5 = (bf16[128,2048]{1,0:T(8,128)(2,1)S(1)}, bf16[128,2048]{1,0:T(8,128)(2,1)}, u32[]{:S(2)}) copy-start(bf16[128,2048]{1,0:T(8,128)(2,1)} %shard_map.159) | copy-start | bytes 1572868
Sparse Core Ops, SparseCore 0:
  97.6 34.6 all-gather.1

commit v2 on v1

--- a/solution.py
+++ b/solution.py
@@ -14,12 +14,6 @@
 DV = 128
 FF = 512
 TOP = 10
-
-
-def shifted(value, axis, steps):
-    count = lax.axis_size(axis)
-    first, last = (max(0, -steps), min(count, count - steps))
-    return lax.ppermute(value, axis, [(source, source + steps) for source in range(first, last)])
 
 
 BF = jnp.bfloat16
@@ -115,7 +109,7 @@
     for i, (intra, qeff, trans, add) in enumerate(results):
         intra_ref[i] = intra
         qeff_ref[i] = qeff.astype(qeff_ref.dtype)
-        trans_ref[i] = trans
+        trans_ref[i] = trans.astype(trans_ref.dtype)
         add_ref[i] = add
 
 
@@ -125,7 +119,7 @@
     group = heads // HK
     out = jax.ShapeDtypeStruct((heads, length, DV), jnp.float32)
     outb = jax.ShapeDtypeStruct((heads, length, DK), BF)
-    sq = jax.ShapeDtypeStruct((heads, DK, DK), jnp.float32)
+    sq = jax.ShapeDtypeStruct((heads, DK, DK), BF)
     sv = jax.ShapeDtypeStruct((heads, DK, DV), jnp.float32)
     block = lambda a, b: pl.BlockSpec((group, a, b), lambda h: (h, 0, 0))
     rows = pl.BlockSpec((1, group, length), lambda h: (h, 0, 0))
@@ -143,6 +137,153 @@
         out_specs=(block(length, DV), block(length, DK), block(DK, DK), block(DK, DV)),
         cost_estimate=pl.CostEstimate(flops=20 * heads * 2 * length**3, bytes_accessed=8 << 20, transcendentals=heads * length * length),
     )(query, key, value, rate.reshape(HK, group, length), cum.reshape(HK, group, length))
+
+
+def mixer_kernel(
+    pieces, trans_ref, add_ref, init_ref, intra_ref, qeff_ref, gate_ref, gain_ref, weight_ref, stream_ref, norm_ref,
+    mixed_ref, moe_ref, state, leaving, gbuf, rbuf, sbuf,
+    state_send, state_recv, g_send, f_send, g_recv, r_send, r_recv,
+):
+    p = lax.axis_index("ctx")
+    n = lax.axis_size("ctx")
+    heads, length, dv = intra_ref.shape
+    per = heads // pieces
+    cols = weight_ref.shape[1]
+    core = p % 2
+    sibling = p + 1 - 2 * core
+
+    barrier = pltpu.get_barrier_semaphore()
+    for d in range(1, n):
+        pl.semaphore_signal(barrier, inc=1, device_id={"ctx": (p + d) % n}, device_id_type=MESH)
+    pl.semaphore_wait(barrier, n - 1)
+
+    def remote(src, dst, ssem, rsem, device):
+        return pltpu.make_async_remote_copy(
+            src_ref=src, dst_ref=dst, send_sem=ssem, recv_sem=rsem, device_id={"ctx": device}, device_id_type=MESH
+        )
+
+    def state_copy(g):
+        return remote(leaving.at[g], state.at[g], state_send.at[g], state_recv.at[g], (p + 1) % n)
+
+    def g_copy(t, g):
+        device = sibling if t == 0 else (p + 2 * t) % n
+        return remote(gbuf.at[p, g], gbuf.at[p, g], g_send.at[t, g], g_recv.at[p, g], device)
+
+    def forward(q, g):
+        return remote(gbuf.at[q, g], gbuf.at[q, g], f_send.at[q, g], g_recv.at[q, g], sibling)
+
+    def r_copy(q):
+        return remote(sbuf.at[q], rbuf.at[p], r_send.at[q], r_recv.at[p], q)
+
+    def r_arrival(q):
+        return remote(sbuf.at[q], rbuf.at[q], r_send.at[q], r_recv.at[q], q)
+
+    for g in range(pieces):
+        @pl.when(p == 0)
+        def _():
+            state[g] = init_ref[g * per : (g + 1) * per].astype(BF)
+
+        @pl.when(p > 0)
+        def _():
+            state_copy(g).wait_recv()
+
+        @pl.when(p < n - 1)
+        def _():
+            for j in range(per):
+                h = g * per + j
+                leaving[g, j] = (mm(trans_ref[h], state[g, j]) + add_ref[h]).astype(BF)
+            state_copy(g).start()
+
+        for j in range(per):
+            h = g * per + j
+            out = intra_ref[h] + mm(qeff_ref[h], state[g, j])
+            out = out * lax.rsqrt(jnp.mean(out * out, axis=-1, keepdims=True) + 1e-06) * gain_ref[...]
+            gate = gate_ref[:, h * dv : (h + 1) * dv].astype(jnp.float32)
+            gbuf[p, g, :, j * dv : (j + 1) * dv] = (out * (gate / (1.0 + jnp.exp(-gate)))).astype(BF)
+        for t in range(n // 2):
+            g_copy(t, g).start()
+
+    for q in range(n):
+        for g in range(pieces):
+            @pl.when(p != q)
+            def _():
+                forward(q, g).wait_recv()
+
+                @pl.when(p % 2 == q % 2)
+                def _():
+                    forward(q, g).start()
+
+        block = mm(gbuf[q, 0], weight_ref[0 : per * dv, :])
+        for g in range(1, pieces):
+            block += mm(gbuf[q, g], weight_ref[g * per * dv : (g + 1) * per * dv, :])
+
+        @pl.when(p == q)
+        def _():
+            rbuf[q] = block.astype(BF)
+
+        @pl.when(p != q)
+        def _():
+            sbuf[q] = block.astype(BF)
+            r_copy(q).start()
+
+    square = jnp.zeros((length, 1), jnp.float32)
+    for q in range(n):
+        @pl.when(p != q)
+        def _():
+            r_arrival(q).wait_recv()
+
+        here = slice(q * cols, (q + 1) * cols)
+        mixed = (stream_ref[:, here].astype(jnp.float32) + rbuf[q].astype(jnp.float32)).astype(BF)
+        mixed_ref[:, here] = mixed
+        mixed = mixed.astype(jnp.float32)
+        square += jnp.sum(mixed * mixed, axis=-1, keepdims=True)
+    scale = lax.rsqrt(square / (n * cols) + 1e-06)
+    for q in range(n):
+        here = slice(q * cols, (q + 1) * cols)
+        moe_ref[:, here] = (mixed_ref[:, here].astype(jnp.float32) * scale * norm_ref[:, here]).astype(BF)
+
+    for g in range(pieces):
+        @pl.when(p < n - 1)
+        def _():
+            state_copy(g).wait_send()
+
+        for t in range(n // 2):
+            g_copy(t, g).wait_send()
+    for q in range(n):
+        @pl.when(p != q)
+        def _():
+            r_copy(q).wait_send()
+
+            @pl.when(p % 2 == q % 2)
+            def _():
+                for g in range(pieces):
+                    forward(q, g).wait_send()
+
+
+def mixer(trans, add, init, intra, qeff, gate, gain, weight, stream, norm):
+    heads, length, dv = intra.shape
+    n = lax.axis_size("ctx")
+    pieces = 4
+    per = heads // pieces
+    cols = weight.shape[1]
+    dma = pltpu.SemaphoreType.DMA
+    return pl.pallas_call(
+        functools.partial(mixer_kernel, pieces),
+        out_shape=(jax.ShapeDtypeStruct(stream.shape, BF), jax.ShapeDtypeStruct(stream.shape, BF)),
+        in_specs=[pl.BlockSpec(memory_space=pltpu.VMEM)] * 10,
+        out_specs=(pl.BlockSpec(memory_space=pltpu.VMEM), pl.BlockSpec(memory_space=pltpu.VMEM)),
+        scratch_shapes=[
+            pltpu.VMEM((pieces, per, DK, dv), BF),
+            pltpu.VMEM((pieces, per, DK, dv), BF),
+            pltpu.VMEM((n, pieces, length, per * dv), BF),
+            pltpu.VMEM((n, length, cols), BF),
+            pltpu.VMEM((n, length, cols), BF),
+            dma((pieces,)), dma((pieces,)),
+            dma((n // 2, pieces)), dma((n, pieces)), dma((n, pieces)),
+            dma((n,)), dma((n,)),
+        ],
+        compiler_params=pltpu.CompilerParams(collective_id=2, has_side_effects=True),
+    )(trans, add, init, intra, qeff, gate, gain.reshape(1, -1), weight, stream, norm.reshape(1, -1))
 
 
 def moe_kernel(
@@ -346,41 +487,14 @@
     expert_up,
     expert_down,
 ):
-    highest = lax.Precision.HIGHEST
     length = stream.shape[1]
     cumulative = jnp.cumsum(log_decay[0], axis=0).T
     intra, query_eff, transit, carry_add = delta_local(
         queries[0], key_proj[0], value_proj[0], write_rate[0].T, cumulative
     )
-    first_state = init_state[0]
-    position = lax.axis_index("ctx")
-
-    def relay_step(turn, start_state):
-        end_state = jnp.einsum("hde,hev->hdv", transit, start_state, precision=highest) + carry_add
-        incoming = shifted(end_state, "ctx", 1)
-        return jnp.where(position == 0, first_state, incoming)
-
-    start_state = lax.fori_loop(0, lax.axis_size("ctx") - 1, relay_step, first_state)
-    head_out = intra + jnp.einsum(
-        "htd,hdv->htv", query_eff, start_state.astype(BF), preferred_element_type=jnp.float32
-    )
-    gate_loc = (
-        gate_proj[0].astype(jnp.float32).reshape(length, OUTPUT_CHANNELS, DV).transpose(1, 0, 2)
-    )
-    square_mean = jnp.mean(head_out * head_out, axis=-1, keepdims=True)
-    gated = head_out * lax.rsqrt(square_mean + 1e-06) * head_gain * jax.nn.silu(gate_loc)
-    gated = gated.transpose(1, 0, 2).reshape(length, OUTPUT_CHANNELS * DV).astype(jnp.bfloat16)
-    column_block = jnp.dot(
-        lax.all_gather(gated, "ctx", axis=0, tiled=True),
-        out_weight,
-        preferred_element_type=jnp.float32,
-    )
-    attn = lax.all_to_all(column_block, "ctx", split_axis=0, concat_axis=1, tiled=True)
-    mixed = (stream[0].astype(jnp.float32) + attn).astype(jnp.bfloat16)
-    mixed_f = mixed.astype(jnp.float32)
-    moe_in = (
-        mixed_f * lax.rsqrt(jnp.mean(mixed_f * mixed_f, axis=-1, keepdims=True) + 1e-06) * moe_gain
-    ).astype(jnp.bfloat16)
+    mixed, moe_in = mixer(
+        transit, carry_add, init_state[0], intra, query_eff, gate_proj[0], head_gain, out_weight, stream[0], moe_gain
+    )
     ctx_count = lax.axis_size("ctx")
     exp_count = lax.axis_size("exp")
     local_experts = expert_up.shape[0]

time: 324 us -> 225 us (0.69)
  waiting for transfers between devices: 76.9 us -> 0 us
  Pallas kernels: 171 us -> 218 us
  matrix products: 17.8 us -> 0.13 us
  local copies, waits for them, and re-layouts: 20.7 us -> 4.24 us
  between operations: 14.1 us -> 0.7 us
  other arithmetic: 12.3 us -> 1.1 us
  starting transfers between devices: 9.05 us -> 0 us
    pallas_call x0 -> x1, Pallas kernels: none -> 38.5 us  [mixer(): pl.pallas_call(functools.partial(mixer_kernel, pieces), out_shape=(jax.Sh...]
    all_gather x1 -> x0, waiting for transfers between devices: 34.8 us -> none  [on_device(): lax.all_gather(gated, 'ctx', axis=0, tiled=True)]
    ppermute x3 -> x0, waiting for transfers between devices: 33.7 us -> none  [shifted(): lax.ppermute(value, axis, [(source, source + steps) for source in range(f...]
    dot_general x5 -> x0, matrix products: 17.6 us -> none  [the longest x3 11 us: relay_step(): jnp.einsum('hde,hev->hdv', transit, start_state, precision=highest)]
    pallas_call x1, Pallas kernels: 151 us -> 160 us  [moe_planes(): pl.pallas_call(functools.partial(moe_kernel, planes, lanes_x), out_shape=...]
    all_to_all x1 -> x0, waiting for transfers between devices: 8.39 us -> none  [on_device(): lax.all_to_all(column_block, 'ctx', split_axis=0, concat_axis=1, tiled=True)]
    convert_element_type x3 -> x0, other arithmetic: 5.49 us -> none  [the longest x1 2.4 us: on_device(): gated.transpose(1, 0, 2).reshape(length, OUTPUT_CHANNELS * DV)]
    all_to_all x1 -> x0, starting transfers between devices: 5.17 us -> none  [on_device(): lax.all_to_all(column_block, 'ctx', split_axis=0, concat_axis=1, tiled=True)]
  transfers between devices with their start and end apart: 5 -> 0, of which waited for: 5 -> 0; matrix products, arithmetic and copies ran while one was open for 1% -> 0% of each run, Pallas kernels for 0% -> 0%
where the time goes in v2:
time: 225 us
  Pallas kernels  218 us (97%)
  local copies, waits for them, and re-layouts  4.24 us (2%)
    pallas_call x1, Pallas kernels, moe_planes(): pl.pallas_call(functools.partial(moe_kernel, planes, lanes_x), out_shape=...  160 us
    pallas_call x1, Pallas kernels, mixer(): pl.pallas_call(functools.partial(mixer_kernel, pieces), out_shape=(jax.Sh...  38.5 us
    pallas_call x1, Pallas kernels, delta_local(): pl.pallas_call(functools.partial(delta_kernel, group), out_shape=(out, ou...  20.1 us

profile of v2, /device:TPU:5, one launch (start us, length us, event | category | flops | bytes accessed | tf_op | source)
XLA Modules:
  0.0 224.6 jit_solution(9302454477398269823)
XLA Ops:
  0.6 0.8 copy.28
  1.4 0.2 reduce_window_sum.11
  1.6 0.7 copy.29
  2.3 20.1 %shard_map.158 = (f32[16,128,128]{2,1,0:T(8,128)}, bf16[16,128,128]{2,1,0:T(8,128)(2,1)}, bf16[16,128,128]{2,1,0:T(8,128)(2,1)}, f32[16,128,128]{2,1,0:T(8,128)}) custom-call(bf16[128,1024]{1,0:T(8,128)(2,1)} %bitcast.63, bf16[128,1024]{1,0:T(8,128)(2,1)} %bitcast.64, bf16[128,2048]{1,0:T(8,128)(2,1)} %bitcast.62, f32[8,2,128]{2,1,0:T(2,128)} %bitcast.65, ...), custom_call_target="tpu_custom_call" | custom-call | flops 1342177280 | bytes 8388608 | tf_op jit(solution)/shard_map/pallas_call | solution.py:126
  22.3 0.0 copy-start.1
  22.3 0.0 copy-start.2
  22.3 38.5 %shard_map.159 = (bf16[128,2048]{1,0:T(8,128)(2,1)}, bf16[128,2048]{1,0:T(8,128)(2,1)}) custom-call(bf16[16,128,128]{2,1,0:T(8,128)(2,1)} %get-tuple-element.8.trans_ref, f32[16,128,128]{2,1,0:T(8,128)} %get-tuple-element.9.add_ref, f32[16,128,128]{2,1,0:T(8,128)} %bitcast.48, f32[16,128,128]{2,1,0:T(8,128)} %get-tuple-element.10.intra_ref, ...), custom_call_target="tpu_custom_call" | custom-call | tf_op jit(solution)/shard_map/pallas_call | solution.py:270
  60.9 0.0 copy-done.1
  60.9 0.1 convolution_select_fusion
  61.1 0.0 copy-done.2
  61.1 0.1 eq.42
  61.2 0.9 fusion.pick_ref
  62.1 0.0 copy-start
  62.1 159.8 %shard_map.160 = bf16[128,2048]{1,0:T(8,128)(2,1)} custom-call(bf16[128,2048]{1,0:T(8,128)(2,1)} %get-tuple-element.13.tok_ref, bf16[4,320,128]{2,1,0:T(8,128)(2,1)} %fusion.pick_ref, bf16[2048,1024]{1,0:T(8,128)(2,1)} %bitcast.45, bf16[512,2048]{1,0:T(8,128)(2,1)} %bitcast.46), custom_call_target="tpu_custom_call" | custom-call | tf_op jit(solution)/shard_map/pallas_call | solution.py:453
  221.9 0.0 copy-done
  221.9 0.8 copy.44
  222.7 1.9 copy.45
  (5 shorter events, 0.1 us)
Async XLA Ops:
  22.3 38.6 %copy-start.1 = (s32[1,128,10]{1,0,2:T(1,128)S(1)}, s32[1,128,10]{1,0,2:T(1,128)}, u32[]{:S(2)}) copy-start(s32[1,128,10]{1,0,2:T(1,128)} %param.26) | copy-start | bytes 15364
  22.3 38.8 %copy-start.2 = (f32[1,128,10]{1,0,2:T(1,128)S(1)}, f32[1,128,10]{1,0,2:T(1,128)}, u32[]{:S(2)}) copy-start(f32[1,128,10]{1,0,2:T(1,128)} %param.27) | copy-start | bytes 15364
  62.1 159.8 %copy-start = (bf16[128,2048]{1,0:T(8,128)(2,1)S(1)}, bf16[128,2048]{1,0:T(8,128)(2,1)}, u32[]{:S(2)}) copy-start(bf16[128,2048]{1,0:T(8,128)(2,1)} %get-tuple-element.12) | copy-start | bytes 1572868

commit v3 on v2

--- a/solution.py
+++ b/solution.py
@@ -58,31 +58,35 @@
     return xs
 
 
-def delta_head(query, keys, values, rate_rows, cum_rows):
-    length = query.shape[0]
+def delta_heads(queries, keys, values, rate_rows, cum_rows):
+    length = queries[0].shape[0]
+    group = len(values) // len(queries)
     rows = lax.broadcasted_iota(jnp.int32, (length, length), 0)
     cols = lax.broadcasted_iota(jnp.int32, (length, length), 1)
     diag = rows == cols
     eye = jnp.where(diag, 1.0, 0.0)
-    query = query.astype(jnp.float32)
-    key = keys.astype(jnp.float32)
-    key = key * lax.rsqrt(jnp.sum(key * key, axis=-1, keepdims=True) + 1e-06)
-    kk = mm_nt(key, key)
-    qk = mm_nt(query, key)
+    units, scores, overlaps = [], [], []
+    for query, key in zip(queries, keys):
+        key = key.astype(jnp.float32)
+        key = key * lax.rsqrt(jnp.sum(key * key, axis=-1, keepdims=True) + 1e-06)
+        units.append(key)
+        overlaps.append(mm_nt(key, key))
+        scores.append(mm_nt(query, key))
     column = lambda row: jnp.sum(jnp.where(diag, row, 0.0), axis=1, keepdims=True)
     lowers, parts = [], []
-    for value, rate_row, cum_row in zip(values, rate_rows, cum_rows):
+    for i, (value, rate_row, cum_row) in enumerate(zip(values, rate_rows, cum_rows)):
         cum, rate = column(cum_row), column(rate_row)
         last = cum_row[:, length - 1 :]
         spread = jnp.exp(jnp.where(rows >= cols, cum - cum_row, 0.0))
-        lowers.append(jnp.where(rows > cols, rate * spread * kk, 0.0))
-        parts.append((value.astype(jnp.float32), cum, rate, last, spread))
+        lowers.append(jnp.where(rows > cols, rate * spread * overlaps[i // group], 0.0))
+        attend = jnp.where(rows >= cols, spread * scores[i // group], 0.0)
+        parts.append((value.astype(jnp.float32), cum, rate, last, attend))
     inverses = unit_lower_inverse(lowers, rows, cols, eye)
     results = []
-    for inverse, (value, cum, rate, last, spread) in zip(inverses, parts):
+    for i, (inverse, (value, cum, rate, last, attend)) in enumerate(zip(inverses, parts)):
+        key, query = units[i // group], queries[i // group].astype(jnp.float32)
         now = jnp.exp(cum)
         solved = mm(inverse, jnp.concatenate([rate * value, (rate * now) * key], axis=1))
-        attend = jnp.where(rows >= cols, spread * qk, 0.0)
         inner = mm(attend, solved)
         tail = mm_tn(jnp.exp(last - cum) * key, solved)
         dv = value.shape[1]
@@ -97,58 +101,19 @@
     return results
 
 
-def delta_kernel(group, q_ref, k_ref, v_ref, rate_ref, cum_ref, intra_ref, qeff_ref, trans_ref, add_ref):
-    width = v_ref.shape[1] // group
-    results = delta_head(
-        q_ref[...],
-        k_ref[...],
-        [v_ref[:, i * width : (i + 1) * width] for i in range(group)],
-        [rate_ref[0, i : i + 1, :] for i in range(group)],
-        [cum_ref[0, i : i + 1, :] for i in range(group)],
-    )
-    for i, (intra, qeff, trans, add) in enumerate(results):
-        intra_ref[i] = intra
-        qeff_ref[i] = qeff.astype(qeff_ref.dtype)
-        trans_ref[i] = trans.astype(trans_ref.dtype)
-        add_ref[i] = add
-
-
-def delta_local(query, key, value, rate, cum):
-    length = query.shape[0]
-    heads = rate.shape[0]
-    group = heads // HK
-    out = jax.ShapeDtypeStruct((heads, length, DV), jnp.float32)
-    outb = jax.ShapeDtypeStruct((heads, length, DK), BF)
-    sq = jax.ShapeDtypeStruct((heads, DK, DK), BF)
-    sv = jax.ShapeDtypeStruct((heads, DK, DV), jnp.float32)
-    block = lambda a, b: pl.BlockSpec((group, a, b), lambda h: (h, 0, 0))
-    rows = pl.BlockSpec((1, group, length), lambda h: (h, 0, 0))
-    return pl.pallas_call(
-        functools.partial(delta_kernel, group),
-        out_shape=(out, outb, sq, sv),
-        grid=(HK,),
-        in_specs=[
-            pl.BlockSpec((length, DK), lambda h: (0, h)),
-            pl.BlockSpec((length, DK), lambda h: (0, h)),
-            pl.BlockSpec((length, group * DV), lambda h: (0, h)),
-            rows,
-            rows,
-        ],
-        out_specs=(block(length, DV), block(length, DK), block(DK, DK), block(DK, DV)),
-        cost_estimate=pl.CostEstimate(flops=20 * heads * 2 * length**3, bytes_accessed=8 << 20, transcendentals=heads * length * length),
-    )(query, key, value, rate.reshape(HK, group, length), cum.reshape(HK, group, length))
-
-
 def mixer_kernel(
-    pieces, trans_ref, add_ref, init_ref, intra_ref, qeff_ref, gate_ref, gain_ref, weight_ref, stream_ref, norm_ref,
-    mixed_ref, moe_ref, state, leaving, gbuf, rbuf, sbuf,
-    state_send, state_recv, g_send, f_send, g_recv, r_send, r_recv,
+    pieces, query_ref, key_ref, value_ref, rate_ref, cum_ref, init_ref, gate_ref, gain_ref, weight_hbm, stream_ref,
+    norm_ref, mixed_ref, moe_ref, state, leaving, gbuf, rbuf, sbuf, weight_ref, weight_sem, state_send, state_recv, g_send, f_send, g_recv, r_send, r_recv,
 ):
     p = lax.axis_index("ctx")
     n = lax.axis_size("ctx")
-    heads, length, dv = intra_ref.shape
+    heads, dv = init_ref.shape[0], init_ref.shape[2]
+    length = query_ref.shape[0]
     per = heads // pieces
+    shared = HK // pieces
     cols = weight_ref.shape[1]
+    fetch = pltpu.make_async_copy(weight_hbm, weight_ref, weight_sem)
+    fetch.start()
     core = p % 2
     sibling = p + 1 - 2 * core
 
@@ -178,10 +143,21 @@
     def r_arrival(q):
         return remote(sbuf.at[q], rbuf.at[q], r_send.at[q], r_recv.at[q], q)
 
-    for g in range(pieces):
+    def piece(g, carry):
+        qcols = [pl.ds(pl.multiple_of((g * shared + j) * DK, DK), DK) for j in range(shared)]
+        vcols = [pl.ds(pl.multiple_of((g * per + j) * dv, dv), dv) for j in range(per)]
+        results = delta_heads(
+            [query_ref[:, c] for c in qcols],
+            [key_ref[:, c] for c in qcols],
+            [value_ref[:, c] for c in vcols],
+            [rate_ref[g, j : j + 1, :] for j in range(per)],
+            [cum_ref[g, j : j + 1, :] for j in range(per)],
+        )
+
         @pl.when(p == 0)
         def _():
-            state[g] = init_ref[g * per : (g + 1) * per].astype(BF)
+            for j in range(per):
+                state[g, j] = init_ref[g * per + j].astype(BF)
 
         @pl.when(p > 0)
         def _():
@@ -190,18 +166,20 @@
         @pl.when(p < n - 1)
         def _():
             for j in range(per):
-                h = g * per + j
-                leaving[g, j] = (mm(trans_ref[h], state[g, j]) + add_ref[h]).astype(BF)
+                leaving[g, j] = (mm(results[j][2], state[g, j]) + results[j][3]).astype(BF)
             state_copy(g).start()
 
         for j in range(per):
-            h = g * per + j
-            out = intra_ref[h] + mm(qeff_ref[h], state[g, j])
+            out = results[j][0] + mm(results[j][1], state[g, j])
             out = out * lax.rsqrt(jnp.mean(out * out, axis=-1, keepdims=True) + 1e-06) * gain_ref[...]
-            gate = gate_ref[:, h * dv : (h + 1) * dv].astype(jnp.float32)
+            gate = gate_ref[:, vcols[j]].astype(jnp.float32)
             gbuf[p, g, :, j * dv : (j + 1) * dv] = (out * (gate / (1.0 + jnp.exp(-gate)))).astype(BF)
         for t in range(n // 2):
             g_copy(t, g).start()
+        return carry
+
+    lax.fori_loop(0, pieces, piece, 0)
+    fetch.wait()
 
     for q in range(n):
         for g in range(pieces):
@@ -260,35 +238,42 @@
                     forward(q, g).wait_send()
 
 
-def mixer(trans, add, init, intra, qeff, gate, gain, weight, stream, norm):
-    heads, length, dv = intra.shape
+def mixer(query, key, value, rate, cum, init, gate, gain, weight, stream, norm):
+    heads, _, dv = init.shape
+    length = query.shape[0]
     n = lax.axis_size("ctx")
-    pieces = 4
+    pieces = HK // 2
     per = heads // pieces
     cols = weight.shape[1]
     dma = pltpu.SemaphoreType.DMA
+    vmem = pl.BlockSpec(memory_space=pltpu.VMEM)
     return pl.pallas_call(
         functools.partial(mixer_kernel, pieces),
         out_shape=(jax.ShapeDtypeStruct(stream.shape, BF), jax.ShapeDtypeStruct(stream.shape, BF)),
-        in_specs=[pl.BlockSpec(memory_space=pltpu.VMEM)] * 10,
-        out_specs=(pl.BlockSpec(memory_space=pltpu.VMEM), pl.BlockSpec(memory_space=pltpu.VMEM)),
+        in_specs=[vmem] * 8 + [pl.BlockSpec(memory_space=pl.ANY)] + [vmem] * 2,
+        out_specs=(vmem, vmem),
         scratch_shapes=[
             pltpu.VMEM((pieces, per, DK, dv), BF),
             pltpu.VMEM((pieces, per, DK, dv), BF),
             pltpu.VMEM((n, pieces, length, per * dv), BF),
             pltpu.VMEM((n, length, cols), BF),
             pltpu.VMEM((n, length, cols), BF),
+            pltpu.VMEM(weight.shape, BF),
+            dma(()),
             dma((pieces,)), dma((pieces,)),
             dma((n // 2, pieces)), dma((n, pieces)), dma((n, pieces)),
             dma((n,)), dma((n,)),
         ],
         compiler_params=pltpu.CompilerParams(collective_id=2, has_side_effects=True),
-    )(trans, add, init, intra, qeff, gate, gain.reshape(1, -1), weight, stream, norm.reshape(1, -1))
+    )(
+        query, key, value, rate.reshape(pieces, per, length), cum.reshape(pieces, per, length), init, gate,
+        gain.reshape(1, -1), weight, stream, norm.reshape(1, -1),
+    )
 
 
 def moe_kernel(
-    planes, lanes_x, tok_ref, pick_ref, up_ref, down_ref, out_ref,
-    tokbuf, pickbuf, sendbuf, recvbuf, prodbuf, retbuf, partbuf, zbuf, total,
+    planes, lanes_x, tok_ref, pick_ref, up_hbm, down_hbm, out_ref,
+    up_ref, down_ref, w_sem, tokbuf, pickbuf, sendbuf, recvbuf, prodbuf, retbuf, partbuf, zbuf, total,
     tok_send, tok_recv, pick_send, pick_recv, d_send, d_recv, r_send, r_recv, z_send, z_recv,
 ):
     c = lax.axis_index("ctx")
@@ -301,6 +286,12 @@
     slots = sendbuf.shape[2]
     width = tok_ref.shape[1]
     ff = down_ref.shape[0]
+    fetches = (
+        pltpu.make_async_copy(up_hbm, up_ref, w_sem.at[0]),
+        pltpu.make_async_copy(down_hbm, down_ref, w_sem.at[1]),
+    )
+    for fetch in fetches:
+        fetch.start()
 
     def plane_device(q):
         return (q // lanes_x, z * lanes_x + q % lanes_x)
@@ -369,9 +360,14 @@
                 d_copy(s, (mine + d) % peers).start()
             recvbuf[s, mine] = sendbuf[s, mine]
 
-        @pl.when((i >= 1) & (i < planes + 1))
-        def _():
-            s = step_of(i - 1)
+        @pl.when(i == 2)
+        def _():
+            for fetch in fetches:
+                fetch.wait()
+
+        @pl.when((i >= 2) & (i < planes + 2))
+        def _():
+            s = step_of((i - 1) % planes)
             for d in range(1, peers):
                 d_arrival(s, (mine + d) % peers).wait_recv()
             rows = recvbuf[s].astype(jnp.float32).reshape(peers * slots, width).astype(BF)
@@ -383,26 +379,26 @@
                 r_copy(s, (mine + d) % peers).start()
             retbuf[s, mine] = prodbuf[s, mine]
 
-        @pl.when(i >= 2)
-        def _():
-            s = step_of(i - 2)
+        @pl.when(i >= 3)
+        def _():
+            s = step_of((i - 2) % planes)
             for d in range(1, peers):
                 r_arrival(s, (mine + d) % peers).wait_recv()
             rows = retbuf[s].astype(jnp.float32).reshape(peers * slots, width).astype(BF)
             part = mm_tn(pickbuf[s], rows)
 
-            @pl.when(i == 2)
+            @pl.when(i == planes + 2)
             def _():
                 total[...] = part
 
-            @pl.when(i > 2)
+            @pl.when(i < planes + 2)
             def _():
                 partbuf[s] = part.astype(BF)
                 z_copy(s).start()
 
         return carry
 
-    lax.fori_loop(0, planes + 2, body, 0)
+    lax.fori_loop(0, planes + 3, body, 0)
 
     for s in range(1, planes):
         z_copy(s).wait_recv()
@@ -453,9 +449,12 @@
     return pl.pallas_call(
         functools.partial(moe_kernel, planes, lanes_x),
         out_shape=jax.ShapeDtypeStruct((length, width), BF),
-        in_specs=[pl.BlockSpec(memory_space=pltpu.VMEM)] * 4,
+        in_specs=[pl.BlockSpec(memory_space=pltpu.VMEM)] * 2 + [pl.BlockSpec(memory_space=pl.ANY)] * 2,
         out_specs=pl.BlockSpec(memory_space=pltpu.VMEM),
         scratch_shapes=[
+            pltpu.VMEM(expert_up.shape[1:], BF),
+            pltpu.VMEM(expert_down.shape[1:], BF),
+            dma((2,)),
             block,
             pltpu.VMEM((planes, peers * slots, length), BF),
             rows_shape, rows_shape, rows_shape, rows_shape,
@@ -489,11 +488,9 @@
 ):
     length = stream.shape[1]
     cumulative = jnp.cumsum(log_decay[0], axis=0).T
-    intra, query_eff, transit, carry_add = delta_local(
-        queries[0], key_proj[0], value_proj[0], write_rate[0].T, cumulative
-    )
     mixed, moe_in = mixer(
-        transit, carry_add, init_state[0], intra, query_eff, gate_proj[0], head_gain, out_weight, stream[0], moe_gain
+        queries[0], key_proj[0], value_proj[0], write_rate[0].T, cumulative, init_state[0], gate_proj[0],
+        head_gain, out_weight, stream[0], moe_gain,
     )
     ctx_count = lax.axis_size("ctx")
     exp_count = lax.axis_size("exp")

time: 225 us -> 194 us (0.86)
  Pallas kernels: 218 us -> 186 us
    pallas_call x1 -> x0, Pallas kernels: 20.1 us -> none  [delta_local(): pl.pallas_call(functools.partial(delta_kernel, group), out_shape=(out, ou...]
    pallas_call x1, Pallas kernels: 160 us -> 146 us  [moe_planes(): pl.pallas_call(functools.partial(moe_kernel, planes, lanes_x), out_shape=...]
where the time goes in v3:
time: 194 us
  Pallas kernels  186 us (96%)
  local copies, waits for them, and re-layouts  5.63 us (3%)
    pallas_call x1, Pallas kernels, moe_planes(): pl.pallas_call(functools.partial(moe_kernel, planes, lanes_x), out_shape=...  146 us
    pallas_call x1, Pallas kernels, mixer(): pl.pallas_call(functools.partial(mixer_kernel, pieces), out_shape=(jax.Sh...  40.5 us
    unnamed x6, local copies, waits for them, and re-layouts  4.07 us

profile of v3, /device:TPU:5, one launch (start us, length us, event | category | flops | bytes accessed | tf_op | source)
XLA Modules:
  0.0 193.8 jit_solution(11704424689684678172)
XLA Ops:
  0.6 0.1 eq.42
  0.7 0.7 copy.41
  1.5 0.7 copy.40
  2.2 0.1 convolution_select_fusion
  2.3 0.8 copy.28
  3.1 0.2 reduce_window_sum.11
  3.3 0.7 copy.29
  3.9 0.9 fusion.pick_ref
  4.8 40.5 %shard_map.158 = (bf16[128,2048]{1,0:T(8,128)(2,1)}, bf16[128,2048]{1,0:T(8,128)(2,1)}) custom-call(bf16[128,1024]{1,0:T(8,128)(2,1)} %bitcast.54, bf16[128,1024]{1,0:T(8,128)(2,1)} %bitcast.55, bf16[128,2048]{1,0:T(8,128)(2,1)} %bitcast.50, f32[4,4,128]{2,1,0:T(4,128)} %bitcast.62, f32[4,4,128]{2,1,0:T(4,128)} %bitcast.58, f32[16,128,128]{2,1,0:T(8,128)} %bitcast.48, ...), custom_call_target="tpu_custom_call" | custom-call | tf_op jit(solution)/shard_map/pallas_call | solution.py:250
  45.3 0.0 copy-start
  45.3 145.8 %shard_map.159 = bf16[128,2048]{1,0:T(8,128)(2,1)} custom-call(bf16[128,2048]{1,0:T(8,128)(2,1)} %get-tuple-element.5.tok_ref, bf16[4,320,128]{2,1,0:T(8,128)(2,1)} %fusion.pick_ref, bf16[2048,1024]{1,0:T(8,128)(2,1)} %bitcast.45, bf16[512,2048]{1,0:T(8,128)(2,1)} %bitcast.46), custom_call_target="tpu_custom_call" | custom-call | tf_op jit(solution)/shard_map/pallas_call | solution.py:449
  191.1 0.0 copy-done
  191.1 0.8 copy.44
  191.9 1.9 copy.45
  (3 shorter events, 0.1 us)
Async XLA Ops:
  45.3 145.8 %copy-start = (bf16[128,2048]{1,0:T(8,128)(2,1)S(1)}, bf16[128,2048]{1,0:T(8,128)(2,1)}, u32[]{:S(2)}) copy-start(bf16[128,2048]{1,0:T(8,128)(2,1)} %get-tuple-element.4) | copy-start | bytes 1572868

commit v4 on v3

--- a/solution.py
+++ b/solution.py
@@ -274,7 +274,7 @@
 def moe_kernel(
     planes, lanes_x, tok_ref, pick_ref, up_hbm, down_hbm, out_ref,
     up_ref, down_ref, w_sem, tokbuf, pickbuf, sendbuf, recvbuf, prodbuf, retbuf, partbuf, zbuf, total,
-    tok_send, tok_recv, pick_send, pick_recv, d_send, d_recv, r_send, r_recv, z_send, z_recv,
+    own_send, tok_send, tok_recv, pick_send, pick_recv, d_send, d_recv, r_send, r_recv, z_send, z_recv,
 ):
     c = lax.axis_index("ctx")
     e = lax.axis_index("exp")
@@ -311,11 +311,30 @@
             src_ref=src, dst_ref=dst, send_sem=ssem, recv_sem=rsem, device_id=device, device_id_type=MESH
         )
 
-    def step_of(i):
-        return (i % 2) * ((i + 1) // 2) + (1 - i % 2) * ((planes - i // 2) % planes)
-
-    def tok_copy(s):
-        return remote(tok_ref, tokbuf.at[s], tok_send.at[s], tok_recv.at[s], line_device((z + s) % planes))
+    fewer = jnp.where(2 * z < planes, z, planes - 1 - z)
+
+    def place(k):
+        paired = k <= 2 * fewer
+        distance = jnp.where(paired, (k + 1) // 2, k - fewer)
+        lower = jnp.where(paired, k % 2 == 1, 2 * z >= planes)
+        return lower, jnp.where(k == 0, 0, jnp.where(lower, distance, planes - distance))
+
+    def step_of(k):
+        return place(k)[1]
+
+    def tok_up(s):
+        return remote(tokbuf.at[s], tokbuf.at[s + 1], tok_send.at[s], tok_recv.at[s + 1], line_device((z + 1) % planes))
+
+    def tok_down(s):
+        return remote(
+            tokbuf.at[s], tokbuf.at[s - 1], tok_send.at[s], tok_recv.at[s - 1], line_device((z + planes - 1) % planes)
+        )
+
+    own_up = remote(tok_ref, tokbuf.at[1], own_send.at[0], tok_recv.at[1], line_device((z + 1) % planes))
+    own_down = remote(
+        tok_ref, tokbuf.at[planes - 1], own_send.at[1], tok_recv.at[planes - 1],
+        line_device((z + planes - 1) % planes),
+    )
 
     def pick_copy(s):
         there = (z + s) % planes
@@ -336,10 +355,16 @@
     def z_copy(s):
         return remote(partbuf.at[s], zbuf.at[s], z_send.at[s], z_recv.at[s], line_device((z - s + planes) % planes))
 
-    for i in range(1, planes):
-        s = (i + 1) // 2 if i % 2 else (planes - i // 2) % planes
+    @pl.when(z + 1 < planes)
+    def _():
+        own_up.start()
+
+    @pl.when(z > 0)
+    def _():
+        own_down.start()
+
+    for s in range(1, planes):
         pick_copy(s).start()
-        tok_copy(s).start()
     tokbuf[0] = tok_ref[...]
     pickbuf[0] = pick_ref[z]
 
@@ -350,8 +375,18 @@
 
             @pl.when(i > 0)
             def _():
+                lower = place(i)[0]
+                tok_up(s - 1).wait_recv()
+
+                @pl.when(lower & (z + 1 < planes))
+                def _():
+                    tok_up(s).start()
+
+                @pl.when(jnp.logical_not(lower) & (z > 0))
+                def _():
+                    tok_down(s).start()
+
                 pick_copy(s).wait_recv()
-                tok_copy(s).wait_recv()
 
             chosen = jnp.where(pickbuf[s].astype(jnp.float32) != 0.0, 1.0, 0.0).astype(BF)
             rows = mm(chosen, tokbuf[s])
@@ -405,8 +440,23 @@
         total[...] += zbuf[s].astype(jnp.float32)
     out_ref[...] = total[...].astype(out_ref.dtype)
 
+    @pl.when(z + 1 < planes)
+    def _():
+        own_up.wait_send()
+
+    @pl.when(z > 0)
+    def _():
+        own_down.wait_send()
+
     for s in range(1, planes):
-        tok_copy(s).wait_send()
+        @pl.when((s <= z) & (z + 1 < planes))
+        def _():
+            tok_up(s).wait_send()
+
+        @pl.when((s > z) & (z > 0))
+        def _():
+            tok_down(s).wait_send()
+
         pick_copy(s).wait_send()
         z_copy(s).wait_send()
 
@@ -461,7 +511,7 @@
             block,
             block,
             pltpu.VMEM((length, width), jnp.float32),
-            dma((planes,)), dma((planes,)), dma((planes,)), dma((planes,)),
+            dma((2,)), dma((planes,)), dma((planes,)), dma((planes,)), dma((planes,)),
             dma((planes, peers)), dma((planes, peers)), dma((planes, peers)), dma((planes, peers)),
             dma((planes,)), dma((planes,)),
         ],

time: 194 us -> 191 us (0.985)
  the two profiles are of different devices: /device:TPU:5 before, /device:TPU:25 now
where the time goes in v4:
time: 191 us; the launch traced here: 190 us
  Pallas kernels  183 us (96%)
  local copies, waits for them, and re-layouts  5.63 us (3%)
    pallas_call x1, Pallas kernels, moe_planes(): pl.pallas_call(functools.partial(moe_kernel, planes, lanes_x), out_shape=...  144 us
    pallas_call x1, Pallas kernels, mixer(): pl.pallas_call(functools.partial(mixer_kernel, pieces), out_shape=(jax.Sh...  38.8 us
    unnamed x6, local copies, waits for them, and re-layouts  4.07 us

profile of v4, /device:TPU:25, one launch (start us, length us, event | category | flops | bytes accessed | tf_op | source)
XLA Modules:
  0.0 190.2 jit_solution(9528097150492498024)
XLA Ops:
  0.6 0.1 eq.42
  0.7 0.7 copy.41
  1.5 0.7 copy.40
  2.2 0.1 convolution_select_fusion
  2.3 0.8 copy.28
  3.1 0.2 reduce_window_sum.11
  3.3 0.7 copy.29
  3.9 0.9 fusion.pick_ref
  4.8 38.8 %shard_map.158 = (bf16[128,2048]{1,0:T(8,128)(2,1)}, bf16[128,2048]{1,0:T(8,128)(2,1)}) custom-call(bf16[128,1024]{1,0:T(8,128)(2,1)} %bitcast.54, bf16[128,1024]{1,0:T(8,128)(2,1)} %bitcast.55, bf16[128,2048]{1,0:T(8,128)(2,1)} %bitcast.50, f32[4,4,128]{2,1,0:T(4,128)} %bitcast.62, f32[4,4,128]{2,1,0:T(4,128)} %bitcast.58, f32[16,128,128]{2,1,0:T(8,128)} %bitcast.48, ...), custom_call_target="tpu_custom_call" | custom-call | tf_op jit(solution)/shard_map/pallas_call | solution.py:250
  43.6 0.0 copy-start
  43.6 143.9 %shard_map.159 = bf16[128,2048]{1,0:T(8,128)(2,1)} custom-call(bf16[128,2048]{1,0:T(8,128)(2,1)} %get-tuple-element.5.tok_ref, bf16[4,320,128]{2,1,0:T(8,128)(2,1)} %fusion.pick_ref, bf16[2048,1024]{1,0:T(8,128)(2,1)} %bitcast.45, bf16[512,2048]{1,0:T(8,128)(2,1)} %bitcast.46), custom_call_target="tpu_custom_call" | custom-call | tf_op jit(solution)/shard_map/pallas_call | solution.py:499
  187.5 0.0 copy-done
  187.6 0.8 copy.44
  188.3 1.9 copy.45
  (3 shorter events, 0.1 us)
Async XLA Ops:
  43.6 143.9 %copy-start = (bf16[128,2048]{1,0:T(8,128)(2,1)S(1)}, bf16[128,2048]{1,0:T(8,128)(2,1)}, u32[]{:S(2)}) copy-start(bf16[128,2048]{1,0:T(8,128)(2,1)} %get-tuple-element.4) | copy-start | bytes 1572868
